TPU v7x, 32 devices: a whole 2x2x4 slice. The times are simulated.
32 devices in a mesh: grp: 8 (over y, x, core), dev: 4 (over z).
Axes of the slice: x: 2, y: 2, z: 4, core: 2. Of those that a mesh axis runs over, the one named last changes fastest.
Arguments:
- tile_patches: bfloat16 [6144, 588], P(('grp', 'dev')), may hold values from -6 to 6
- w_patch: bfloat16 [588, 1536], replicated, may hold values from -0.25 to 0.25
- w_tqkv: bfloat16 [3, 1536, 1536], P(None, None, 'dev'), may hold values from -6 to 6
- w_to: bfloat16 [1536, 1536], P('dev'), may hold values from -0.15625 to 0.15625
- w_gu: bfloat16 [2, 1536, 4096], P(None, None, 'dev'), may hold values from -0.15625 to 0.15625
- w_down: bfloat16 [4096, 1536], P('dev'), may hold values from -0.09375 to 0.09375
- tile_gain: float32 [3, 1536], replicated, may hold values from 0.1 to 1.9
- w_in: bfloat16 [1536, 768], replicated, may hold values from -0.15625 to 0.15625
- slide_tokens: bfloat16 [65536, 768], P(('grp', 'dev')), may hold values from -6 to 6
- slide_gain: float32 [768], replicated, may hold values from 0.1 to 1.9
- w_sqkv: bfloat16 [3, 768, 768], replicated, may hold values from -6 to 6
- w_so: bfloat16 [768, 768], replicated, may hold values from -1.75 to 1.75
- pattern_of_group: int32 [4], replicated, may hold values from 0 to 3, each once
- new_positions: int32 [24], replicated, may hold values from 0 to 65535, as said below
Outputs:
- tile_embed: bfloat16 [24, 768], P('grp')
- slide_out: bfloat16 [65536, 768], P(('grp', 'dev'))
Inputs may be any that keep to these rules, and one draw needn't show every extreme that they name: `pattern_of_group`: each of the four patterns is used by exactly one head group. `new_positions`: distinct positions.
All inputs are finite; a program needn't handle non-finite values.
Results may differ from a plain program's by a relative error of at most 0.025.
Values may be sent and summed in bfloat16 or wider, within the bound.
No kernel may reach another device: no remote copies, remote signals or barrier semaphores. Data moves between devices by JAX's collectives and lax.ppermute only.
A program may use at most 256 MiB of HBM per device.

v0:
```python
import functools
import math

import jax
import jax.numpy as jnp
from jax import lax
from jax.experimental import pallas as pl
from jax.experimental.pallas import tpu as pltpu
from jax.sharding import PartitionSpec as P


TILE_HEAD = 64
PATCHES = 256
SLIDE_HEAD = 48
GROUPS = 4
MASKED = -1e30
LOG2E = math.log2(math.e)
F32 = jnp.float32
BF16 = jnp.bfloat16
VMEM_LIMIT = 60 * 1024 * 1024


def norm(x, gain):
    center = x - jnp.mean(x, axis=-1, keepdims=True)
    spread = jnp.mean(center * center, axis=-1, keepdims=True)
    return center * lax.rsqrt(spread + 1e-06) * gain


def mm(a, b):
    return jnp.dot(a, b, preferred_element_type=F32)


def mmt(a, b):
    return lax.dot_general(a, b, (((1,), (1,)), ((), ())), preferred_element_type=F32)


def lanes(shape):
    return lax.broadcasted_iota(jnp.int32, shape, len(shape) - 1)


def params(**kw):
    return pltpu.CompilerParams(vmem_limit_bytes=VMEM_LIMIT, **kw)


def cost(flops, bytes_accessed, trans=0):
    return pl.CostEstimate(flops=int(flops), bytes_accessed=int(bytes_accessed), transcendentals=int(trans))


def whole(shape):
    return pl.BlockSpec(shape, lambda *_: (0,) * len(shape))


def tile_front_kernel(devs, where_ref, *rest):
    patch_refs = rest[:devs]
    wp_ref, wqkv_ref, gain_ref, x0_ref, att_ref, held = rest[devs:]
    step = pl.program_id(0)

    @pl.when(step == 0)
    def _():
        count = patch_refs[0].shape[0]
        for k in range(devs):
            held[pl.ds(pl.multiple_of(where_ref[k] * count, count), count), :] = patch_refs[k][...]

    patch = held[pl.ds(pl.multiple_of(step * PATCHES, PATCHES), PATCHES), :]
    x0 = mm(patch, wp_ref[...]).astype(BF16)
    x0_ref[...] = x0
    h1 = norm(x0.astype(F32), gain_ref[0:1, :]).astype(BF16)
    q = (mm(h1, wqkv_ref[0]) * (TILE_HEAD ** -0.5 * LOG2E)).astype(BF16)
    k = mm(h1, wqkv_ref[1]).astype(BF16)
    v = mm(h1, wqkv_ref[2]).astype(BF16)
    width = 2 * TILE_HEAD
    first = lanes((PATCHES, width)) < TILE_HEAD
    for pair in range(q.shape[1] // width):
        cut = slice(pair * width, (pair + 1) * width)
        qp, kp, vp = q[:, cut], k[:, cut], v[:, cut]
        none = jnp.zeros_like(qp)
        both = []
        for s in (mmt(jnp.where(first, qp, none), kp), mmt(jnp.where(first, none, qp), kp)):
            e = jnp.exp2(s - jnp.max(s, axis=1, keepdims=True))
            total = jnp.sum(e, axis=1, keepdims=True)
            both.append(mm(e.astype(BF16), vp) / total)
        att_ref[:, cut] = jnp.where(first, both[0], both[1]).astype(BF16)


def tile_front(where, patches, w_patch, w_tqkv, gain):
    devs = len(patches)
    count, vec = patches[0].shape
    tokens = devs * count
    width = w_patch.shape[1]
    part = w_tqkv.shape[2]
    return pl.pallas_call(
        functools.partial(tile_front_kernel, devs),
        grid=(tokens // PATCHES,),
        in_specs=[pl.BlockSpec(memory_space=pltpu.SMEM)]
        + [whole((count, vec))] * devs
        + [
            whole(w_patch.shape),
            whole(w_tqkv.shape),
            whole(gain.shape),
        ],
        out_specs=[
            pl.BlockSpec((PATCHES, width), lambda i: (i, 0)),
            pl.BlockSpec((PATCHES, part), lambda i: (i, 0)),
        ],
        out_shape=[
            jax.ShapeDtypeStruct((tokens, width), BF16),
            jax.ShapeDtypeStruct((tokens, part), BF16),
        ],
        scratch_shapes=[pltpu.VMEM((tokens, vec), BF16)],
        compiler_params=params(),
        cost_estimate=cost(2 * tokens * width * (vec + 3 * part), 2 * (width * (vec + 3 * part) + tokens * (vec + width + part))),
        name="tile_front",
    )(where, *patches, w_patch, w_tqkv, gain)


def tile_back_kernel(devs, pieces, x0_ref, *rest):
    att_refs = rest[: 2 * devs - 1]
    rest = rest[2 * devs - 1 :]
    far_refs = rest[:pieces]
    (wto_own, wgu_any, wdown_any, gain_ref, order_ref, out_ref, wto, wgu, wdown, hsum, sems) = rest[pieces:]
    step = pl.program_id(0)
    rows = wto_own.shape[0]
    piece = rows // pieces

    def far(k, b):
        place = pl.multiple_of(order_ref[b] * piece, piece)
        return pltpu.make_async_copy(far_refs[b].at[k, pl.ds(0, piece)], wto.at[k, pl.ds(place, piece)], sems.at[k])

    def own():
        return pltpu.make_async_copy(wto_own, wto.at[0], sems.at[0])

    def gu(i):
        return pltpu.make_async_copy(wgu_any.at[i], wgu.at[i], sems.at[devs + i])

    def down():
        return pltpu.make_async_copy(wdown_any, wdown, sems.at[devs + 2])

    @pl.when(step == 0)
    def _():
        own().start()
        for k in range(1, devs):
            for b in range(pieces):
                far(k, b).start()
        gu(0).start()
        gu(1).start()
        down().start()
        hsum[...] = jnp.zeros_like(hsum)
        out_ref[...] = jnp.zeros_like(out_ref)
        own().wait()
        for k in range(1, devs):
            for b in range(pieces):
                far(k, b).wait()

    x1 = x0_ref[...].astype(F32) + mm(att_refs[0][...], wto[0])
    for k in range(1, devs):
        near = order_ref[pieces] >= k
        att = jnp.where(near, att_refs[2 * k - 1][...], att_refs[2 * k][...])
        x1 = x1 + mm(att, wto[k])
    x1 = x1.astype(BF16).astype(F32)
    h2 = norm(x1, gain_ref[1:2, :]).astype(BF16)

    @pl.when(step == 0)
    def _():
        gu(0).wait()
        gu(1).wait()

    gate = mm(h2, wgu[0])
    up = mm(h2, wgu[1])
    hidden = (gate * (1.0 / (1.0 + jnp.exp(-gate))) * up).astype(BF16).astype(F32)
    out_ref[1, pl.ds(step, 1), :] = jnp.mean(x1, axis=0, keepdims=True)
    hsum[pl.ds(step, 1), :] = jnp.mean(hidden, axis=0, keepdims=True)

    @pl.when(step == pl.num_programs(0) - 1)
    def _():
        down().wait()
        high = hsum[...].astype(BF16)
        low = (hsum[...] - high.astype(F32)).astype(BF16)
        out_ref[0] = mm(high, wdown[...]) + mm(low, wdown[...])


def tile_back(x0, atts, wto_own, wto_far, w_gu, w_down, gain, order):
    devs = len(atts)
    atts = atts[:1] + [a for pair in atts[1:] for a in pair]
    pieces = len(wto_far)
    tokens, width = x0.shape
    part = atts[0].shape[1]
    hid = w_gu.shape[2]
    anyspec = pl.BlockSpec(memory_space=pl.ANY)
    return pl.pallas_call(
        functools.partial(tile_back_kernel, devs, pieces),
        grid=(tokens // PATCHES,),
        in_specs=[pl.BlockSpec((PATCHES, width), lambda i: (i, 0))]
        + [pl.BlockSpec((PATCHES, part), lambda i: (i, 0))] * (2 * devs - 1)
        + [anyspec] * (pieces + 3)
        + [whole(gain.shape), pl.BlockSpec(memory_space=pltpu.SMEM)],
        out_specs=whole((2, 8, width)),
        out_shape=jax.ShapeDtypeStruct((2, 8, width), F32),
        scratch_shapes=[
            pltpu.VMEM((devs, part, width), BF16),
            pltpu.VMEM(w_gu.shape, BF16),
            pltpu.VMEM(w_down.shape, BF16),
            pltpu.VMEM((8, hid), F32),
            pltpu.SemaphoreType.DMA((devs + 3,)),
        ],
        compiler_params=params(),
        cost_estimate=cost(2 * tokens * width * (width + 2 * hid), 2 * width * (width + 3 * hid) + 4 * tokens * width),
        name="tile_back",
    )(x0, *atts, *wto_far, wto_own, w_gu, w_down, gain, order)


def embed_kernel(tiles, where_ref, parts_ref, mean_ref, gain_ref, win_ref, out_ref):
    pooled = mean_ref[...]
    for b in range(parts_ref.shape[0]):
        pooled = pooled + parts_ref[where_ref[b]]
    normed = norm(pooled, gain_ref[2:3, :]).astype(BF16)
    out_ref[...] = mm(normed, win_ref[...])[:tiles].astype(BF16)


def embed(where, parts, mean, gain, w_in, tiles):
    return pl.pallas_call(
        functools.partial(embed_kernel, tiles),
        in_specs=[pl.BlockSpec(memory_space=pltpu.SMEM)] + [pl.BlockSpec(memory_space=pltpu.VMEM)] * 4,
        out_specs=pl.BlockSpec(memory_space=pltpu.VMEM),
        out_shape=jax.ShapeDtypeStruct((tiles, w_in.shape[1]), BF16),
        compiler_params=params(),
        cost_estimate=cost(16 * w_in.shape[0] * w_in.shape[1], 2 * w_in.shape[0] * w_in.shape[1]),
        name="tile_embed",
    )(where, parts, mean, gain, w_in)


USED = GROUPS * SLIDE_HEAD
FLAGS = 256 - USED
SHARE = FLAGS // GROUPS


def between(lane, low, count):
    return jnp.logical_and(lane >= low, lane < low + count)


def own_q(lane, h):
    return between(lane, FLAGS + SLIDE_HEAD * h, SLIDE_HEAD)


def own_sum(lane, h):
    return jnp.logical_or(between(lane, SLIDE_HEAD * h, SLIDE_HEAD), between(lane, USED + SHARE * h, SHARE))


def flagged(q):
    return jnp.where(lanes(q.shape) < GROUPS, 1.0, q).astype(BF16)


def one_head(q, lane, h):
    return jnp.where(own_q(lane, h), q, jnp.where(lane == h, 1.0, 0.0).astype(q.dtype))


def slide_proj_kernel(ratios, gid_ref, x_ref, gain_ref, w_any, *rest):
    q_refs = rest[0:4]
    kv0_ref, near_ref, far_ref, w_ref, held = rest[4:9]
    block, width = x_ref.shape
    scale = SLIDE_HEAD ** -0.5 * LOG2E
    step = pl.program_id(0)

    @pl.when(step == 0)
    def _():
        w_ref[:, :, 0:FLAGS] = jnp.zeros((GROUPS, width, FLAGS), BF16)
        for g in range(GROUPS):
            cut = slice(g * USED, (g + 1) * USED)
            w_ref[g, :, FLAGS:256] = w_any[0, :, cut]
            w_ref[g, :, 256 : 256 + USED] = w_any[2, :, cut]
            w_ref[g, :, 256 + USED : 256 + 2 * USED] = w_any[1, :, cut]

    hs = norm(x_ref[...].astype(F32), gain_ref[...]).astype(BF16)
    wide = hs.astype(F32)
    for c in range(held.shape[0]):
        held[c] = wide[:, c * 128 : (c + 1) * 128]
    y = mm(hs, w_ref[gid_ref[0]])
    q_refs[0][...] = flagged(y[:, :256] * scale)
    kv0_ref[...] = y[:, 256:].astype(BF16)
    base = 0
    for p in range(1, 4):
        ratio = ratios[p]
        count = block // ratio
        rows = jnp.concatenate(
            [
                jnp.concatenate(
                    [held[c, pl.ds(j % ratio, count, stride=ratio), :] for j in range(GROUPS)], axis=0
                )
                for c in range(held.shape[0])
            ],
            axis=1,
        ).astype(BF16)
        y = mm(rows, w_ref[gid_ref[p]])
        lane = lanes((count, y.shape[1])) - FLAGS
        kept = y[0:count]
        for j in range(1, GROUPS):
            here = between(lane, SLIDE_HEAD * j, SLIDE_HEAD)
            here = jnp.logical_or(here, between(lane, USED + SLIDE_HEAD * j, SLIDE_HEAD))
            here = jnp.logical_or(here, between(lane, 2 * USED + SLIDE_HEAD * j, SLIDE_HEAD))
            kept = jnp.where(here, y[j * count : (j + 1) * count], kept)
        q_refs[p][...] = flagged(kept[:, :256] * scale)
        if p == 3:
            far_ref[...] = kept[:, 256:].astype(BF16)
        else:
            spot = pl.multiple_of(base + step * count, 16)
            near_ref[pl.ds(spot, count), :] = kept[:, 256:].astype(BF16)
            base = base + count * pl.num_programs(0)


def slide_block(rows, ratios):
    return min(rows, 16 * ratios[3])


def slide_proj(gid, tokens, gain, w, ratios):
    rows, width = tokens.shape
    block = slide_block(rows, ratios)
    counts = [rows // r for r in ratios]
    wide = (GROUPS, width, 256 + 2 * USED)
    return pl.pallas_call(
        functools.partial(slide_proj_kernel, ratios),
        grid_spec=pltpu.PrefetchScalarGridSpec(
            num_scalar_prefetch=1,
            grid=(rows // block,),
            in_specs=[
                pl.BlockSpec((block, width), lambda i, g: (i, 0)),
                whole(gain.shape),
                whole(w.shape),
            ],
            out_specs=[pl.BlockSpec((block // r, 256), lambda i, g: (i, 0)) for r in ratios]
            + [
                pl.BlockSpec((block, 2 * USED), lambda i, g: (i, 0)),
                whole((sum(counts[1:3]), 2 * USED)),
                pl.BlockSpec((block // ratios[3], 2 * USED), lambda i, g: (0, i)),
                whole(wide),
            ],
            scratch_shapes=[pltpu.VMEM((width // 128, block, 128), F32)],
        ),
        out_shape=[jax.ShapeDtypeStruct((c, 256), BF16) for c in counts]
        + [
            jax.ShapeDtypeStruct((rows, 2 * USED), BF16),
            jax.ShapeDtypeStruct((sum(counts[1:3]), 2 * USED), BF16),
            jax.ShapeDtypeStruct((block // ratios[3], rows // block * 2 * USED), BF16),
            jax.ShapeDtypeStruct(wide, BF16),
        ],
        compiler_params=params(),
        cost_estimate=cost(2 * rows * width * 640 * 2.6, 2 * rows * width * 3 + 2 * w.size),
        name="slide_proj",
    )(gid, tokens, gain, w)


def augment(pieces, at, ratio, pos_ref, news, ka, va):
    keys = ka.shape[0]
    head = lax.broadcasted_iota(jnp.int32, (8, keys), 0)
    here = jnp.broadcast_to(at, (8, keys))
    if ratio > 1:
        here = here + head
    low = jnp.zeros((8, keys), F32)
    for n in range(news):
        low = jnp.where(here == pos_ref[n], MASKED, low)
    spread = jnp.where(lanes((8, 256)) == lax.broadcasted_iota(jnp.int32, (8, 256), 0), 1.0, 0.0).astype(BF16)
    low = lax.dot_general(
        low.astype(BF16), spread, (((0,), (0,)), ((), ())), preferred_element_type=F32
    ).astype(BF16)
    spot = 0
    for load in pieces:
        value, key = load()
        count = value.shape[0]
        lane = lanes((count, 256))
        cut = slice(spot, spot + count)
        ka[cut] = jnp.where(lane < FLAGS, low[cut], key)
        va[cut] = jnp.where(lane < USED, value, jnp.ones_like(value))
        spot += count


def state(sums, tops):
    rows = sums.shape[0]
    low = sums[:, 128:256]
    lane = lanes((rows, 128))
    for h in range(GROUPS):
        low = jnp.where(between(lane, USED - 128 + SHARE * h + 8, 8), tops[h], low)
    return jnp.transpose(low)[USED - 128 :]


def attend(q, ka, va):
    rows = q.shape[0]
    lane = lanes(q.shape)
    tops = []
    sums = jnp.zeros((rows, 256), F32)
    s = mmt(one_head(q, lane, 0), ka[...])
    for h in range(GROUPS):
        after = mmt(one_head(q, lane, h + 1), ka[...]) if h + 1 < GROUPS else None
        m = jnp.max(s, axis=1, keepdims=True)
        o = mm(jnp.exp2(s - m).astype(BF16), va[...])
        sums = jnp.where(own_sum(lane, h), o, sums)
        tops.append(m)
        s = after
    return sums, state(sums, tops)


def attend_stacked(q, ka, va):
    rows = q.shape[0]
    lane = lanes(q.shape)
    s = mmt(jnp.concatenate([one_head(q, lane, h) for h in range(GROUPS)], axis=0), ka[...])
    m = jnp.max(s, axis=1, keepdims=True)
    o = mm(jnp.exp2(s - m).astype(BF16), va[...])
    sums = o[0:rows]
    for h in range(1, GROUPS):
        sums = jnp.where(own_sum(lane, h), o[h * rows : (h + 1) * rows], sums)
    return sums, state(sums, [m[h * rows : (h + 1) * rows] for h in range(GROUPS)])


def loaders(refs, cuts):
    made = []
    for ref, cut in zip(refs, cuts):

        def load(ref=ref, cut=cut):
            index = cut[:-2] + (slice(cut[-2][0], cut[-2][1]),)
            lane = cut[-1]
            return ref[index + (slice(lane, lane + 256),)], ref[index + (slice(lane + 128, lane + 384),)]

        made.append(load)
    return made


def slide_attend_kernel(ratio, news, cuts, used, pos_ref, at_ref, q_ref, *rest):
    count = max(used) + 1
    kv_refs = rest[:count]
    sum_ref, top_ref, ka, va = rest[-4:]

    @pl.when(pl.program_id(0) == 0)
    def _():
        augment(loaders([kv_refs[u] for u in used], cuts), at_ref[...], ratio, pos_ref, news, ka, va)

    small = q_ref.shape[0] < 128
    sums, tops = (attend_stacked if small else attend)(q_ref[...], ka, va)
    sum_ref[...] = sums
    if len(top_ref.shape) == 2:
        top_ref[...] = tops
    else:
        size = top_ref.shape[2]
        for u in range(top_ref.shape[0]):
            top_ref[u] = tops[:, u * size : (u + 1) * size]


def slide_attend(pos, at, q, kv, ratio, size, half=None, earlier=()):
    arrays, used, cuts = kv
    rows = q.shape[0]
    keys = at.shape[1]
    block = min(rows, 256)
    steps = rows // block
    first = 0
    if half is not None:
        first, steps = half * (steps // 2), steps // 2
    smem = pl.BlockSpec(memory_space=pltpu.SMEM)
    if block <= size:
        per = size // block
        top_spec = pl.BlockSpec((None, FLAGS, block), lambda i: ((i + first) // per, 0, (i + first) % per))
    else:
        top_spec = pl.BlockSpec((block // size, FLAGS, size), lambda i: (i + first, 0, 0))
    done = steps * block
    return pl.pallas_call(
        functools.partial(slide_attend_kernel, ratio, pos.shape[0], cuts, used),
        grid=(steps,),
        in_specs=[
            smem,
            whole(at.shape),
            pl.BlockSpec((block, 256), lambda i: (i + first, 0)),
        ]
        + [whole(a.shape) for a in arrays]
        + [pl.BlockSpec(memory_space=pl.ANY)] * len(earlier),
        out_specs=[
            pl.BlockSpec((block, 256), lambda i: (i + first, 0)),
            top_spec,
        ],
        out_shape=[
            jax.ShapeDtypeStruct((rows, 256), F32),
            jax.ShapeDtypeStruct((rows // size, FLAGS, size), F32),
        ],
        scratch_shapes=[pltpu.VMEM((keys, 256), BF16), pltpu.VMEM((keys, 256), BF16)],
        input_output_aliases={3 + len(arrays) + i: i for i in range(len(earlier))},
        compiler_params=params(),
        cost_estimate=cost(4 * 4 * done * keys * 256, 2 * keys * 384 + 6 * done * 256, 4 * done * keys),
    )(pos, at, q, *arrays, *earlier)


def fresh_kernel(ratios, news, plan, seg_ref, gid_ref, news_ref, emb_ref, pos_ref, gain_ref, w_ref, at_ref, *rest):
    total = sum(n for n, _, _ in plan)
    kv_refs = rest[:total]
    q_ref, sum_ref, top_ref, ka_ref, va_ref, ka, va = rest[total:]
    scale = SLIDE_HEAD ** -0.5 * LOG2E
    hs = norm(emb_ref[...], gain_ref[...]).astype(BF16)
    slots = emb_ref.shape[0]
    pos = pos_ref[...]
    lane = lanes((slots, 256))
    row = lax.broadcasted_iota(jnp.int32, (slots, 256), 0)
    first = 0
    for p in range(4):
        y = mm(hs, w_ref[gid_ref[p]])
        q = flagged(y[:, :256] * scale)
        kv = y[:, 256:].astype(BF16)
        span = ratios[p] * seg_ref[1]
        same = (pos // span) == (seg_ref[0] // span)
        seen = jnp.broadcast_to(same, lane.shape)
        if ratios[p] > 1:
            seen = jnp.logical_and(seen, lax.rem(pos, ratios[p]) == lane)
        seen = jnp.logical_and(seen, row < news)
        flag = jnp.where(seen, 0.0, MASKED).astype(BF16)
        none = jnp.zeros_like(flag)
        for h in range(GROUPS):
            key = jnp.where(own_q(lane, h), kv[:, 128:384], jnp.where(lane == h, flag, none))
            ka_ref[p, h * slots : (h + 1) * slots] = key
            va_ref[p, h * slots : (h + 1) * slots] = jnp.where(between(lane, SLIDE_HEAD * h, SLIDE_HEAD), kv[:, 0:256], none)
        q_ref[p] = q.astype(F32)
        count, used, cuts = plan[p]
        refs = kv_refs[first : first + count]
        first += count
        augment(loaders([refs[u] for u in used], cuts), at_ref[p], ratios[p], news_ref, news, ka, va)
        sums, tops = attend_stacked(q, ka, va)
        sum_ref[p] = sums
        top_ref[p] = tops


def fresh(seg, gid, news_pos, emb, pos, gain, w, at, kvs, ratios):
    slots = emb.shape[0]
    keys = at.shape[-1]
    smem = pl.BlockSpec(memory_space=pltpu.SMEM)
    vmem = pl.BlockSpec(memory_space=pltpu.VMEM)
    plan = [(len(arrays), used, cuts) for arrays, used, cuts in kvs]
    flat = [a for arrays, _, _ in kvs for a in arrays]
    return pl.pallas_call(
        functools.partial(fresh_kernel, ratios, news_pos.shape[0], plan),
        in_specs=[smem] * 3 + [vmem] * (5 + len(flat)),
        out_specs=[vmem] * 5,
        out_shape=[
            jax.ShapeDtypeStruct((4, slots, 256), F32),
            jax.ShapeDtypeStruct((4, slots, 256), F32),
            jax.ShapeDtypeStruct((4, FLAGS, slots), F32),
            jax.ShapeDtypeStruct((4, GROUPS * slots, 256), BF16),
            jax.ShapeDtypeStruct((4, GROUPS * slots, 256), BF16),
        ],
        scratch_shapes=[pltpu.VMEM((keys, 256), BF16), pltpu.VMEM((keys, 256), BF16)],
        compiler_params=params(),
        cost_estimate=cost(4 * 4 * 4 * slots * keys * 256, 2 * w.size + 8 * keys * 384, 16 * slots * keys),
        name="slide_fresh",
    )(seg, gid, news_pos, emb, pos, gain, w, at, *flat)


def finish_kernel(ratios, news, gid_ref, start_ref, pos_ref, x_ref, emb_ref, wso_ref, *rest):
    q_refs = rest[0:4]
    sum_refs = rest[4:8]
    top_refs = rest[8:12]
    nq_ref, nsum_ref, ntop_ref, nka_ref, nva_ref, out_ref = rest[12:18]
    seq = rest[18]
    qs = rest[19:23]
    ss = rest[23:27]
    ts = rest[27:31]
    placed = rest[31:34]
    step = pl.program_id(0)
    block = x_ref.shape[0]
    start = start_ref[0] + step * block
    seq[...] = x_ref[...].astype(F32)
    for p in range(4):
        qs[p][...] = q_refs[p][...].astype(F32)
        ss[p][...] = sum_refs[p][...]
        ts[p][...] = top_refs[p][...]

    @pl.when(step == 0)
    def _():
        for p in range(1, 4):
            placed[p - 1][...] = jnp.zeros_like(placed[p - 1])

    lane = lanes((1, 256))

    def patch(n, carry):
        row = pos_ref[n] - start

        @pl.when(jnp.logical_and(row >= 0, row < block))
        def _():
            one = pl.ds(n, 1)
            seq[pl.ds(row, 1), :] = emb_ref[one, :]
            for p in range(4):
                spot = row // ratios[p]
                at = pl.ds(spot, 1)
                fresh_state = ntop_ref[p]
                column = jnp.sum(jnp.where(lanes(fresh_state.shape) == n, fresh_state, 0.0), axis=1, keepdims=True)
                held_state = ts[p][...]
                mine = lanes(held_state.shape) == spot
                if ratios[p] == 1:
                    qs[p][at, :] = nq_ref[p, one, :]
                    ss[p][at, :] = nsum_ref[p, one, :]
                else:
                    head = lax.rem(pos_ref[n], ratios[p])
                    fits = head < GROUPS
                    mine_q = jnp.logical_and(own_q(lane, head), fits)
                    mine_sum = jnp.logical_and(own_sum(lane, head), fits)
                    qs[p][at, :] = jnp.where(mine_q, nq_ref[p, one, :], qs[p][at, :])
                    ss[p][at, :] = jnp.where(mine_sum, nsum_ref[p, one, :], ss[p][at, :])
                    line = lax.broadcasted_iota(jnp.int32, held_state.shape, 0)
                    mine = jnp.logical_and(mine, between(line, SHARE * head, SHARE))
                ts[p][...] = jnp.where(mine, column, held_state)

        return carry

    lax.fori_loop(0, news, patch, 0)

    slots = nka_ref.shape[1] // GROUPS
    owner = lanes((24, 256)) // SLIDE_HEAD
    spread = jnp.where(owner == lax.rem(lax.broadcasted_iota(jnp.int32, (24, 256), 0), 8), 1.0, 0.0).astype(BF16)
    result = seq[...]
    for p in range(4):
        count = block // ratios[p]
        s = mmt(nka_ref[p], qs[p][...].astype(BF16))
        weights = []
        scale = jnp.zeros((8, count), F32)
        line = lax.broadcasted_iota(jnp.int32, (8, count), 0)
        for h in range(GROUPS):
            own = s[h * slots : (h + 1) * slots]
            total = ts[p][SHARE * h : SHARE * h + 1]
            old = ts[p][SHARE * h + 8 : SHARE * h + 9]
            top = jnp.maximum(old, jnp.max(own, axis=0, keepdims=True))
            e = jnp.exp2(own - top)
            shrink = jnp.exp2(old - top)
            inverse = 1.0 / (total * shrink + jnp.sum(e, axis=0, keepdims=True))
            weights.append((e * inverse).astype(BF16))
            scale = jnp.where(line == h, shrink * inverse, scale)
        o = lax.dot_general(
            jnp.concatenate(weights, axis=0), nva_ref[p], (((0,), (0,)), ((), ())), preferred_element_type=F32
        )
        high = scale.astype(BF16)
        rest_one = scale - high.astype(F32)
        middle = rest_one.astype(BF16)
        low = (rest_one - middle.astype(F32)).astype(BF16)
        split = jnp.concatenate([high.astype(F32), middle.astype(F32), low.astype(F32)], axis=0).astype(BF16)
        wide = lax.dot_general(split, spread, (((0,), (0,)), ((), ())), preferred_element_type=F32)
        value = ss[p][...] * wide + o
        if ratios[p] == 1:
            att = value[:, :USED].astype(BF16)
        else:
            lane_wide = lanes((count, 256))
            for j in range(GROUPS):
                own = jnp.where(between(lane_wide, SLIDE_HEAD * j, SLIDE_HEAD), value, 0.0)
                for c in range(2):
                    at = pl.ds(j, count, stride=ratios[p])
                    placed[p - 1][c, at, :] = own[:, c * 128 : (c + 1) * 128]
            att = jnp.concatenate([placed[p - 1][0], placed[p - 1][1]], axis=1)[:, :USED].astype(BF16)
        result = result + mm(att, wso_ref[gid_ref[p]])
    out_ref[...] = result.astype(BF16)


def finish(gid, start, pos, tokens, emb, wso, qs, sums, tops, new, ratios, news):
    rows, width = tokens.shape
    block = slide_block(rows, ratios)
    counts = [block // r for r in ratios]

    def rowblock(n, lanes_here):
        return pl.BlockSpec((n, lanes_here), lambda i, *_: (i, 0))

    return pl.pallas_call(
        functools.partial(finish_kernel, ratios, news),
        grid_spec=pltpu.PrefetchScalarGridSpec(
            num_scalar_prefetch=3,
            grid=(rows // block,),
            in_specs=[rowblock(block, width), whole(emb.shape), whole(wso.shape)]
            + [rowblock(c, 256) for c in counts]
            + [rowblock(c, 256) for c in counts]
            + [pl.BlockSpec((None, FLAGS, c), lambda i, *_: (i, 0, 0)) for c in counts]
            + [whole(a.shape) for a in new],
            out_specs=rowblock(block, width),
            scratch_shapes=[pltpu.VMEM((block, width), F32)]
            + [pltpu.VMEM((c, 256), F32) for c in counts]
            + [pltpu.VMEM((c, 256), F32) for c in counts]
            + [pltpu.VMEM((FLAGS, c), F32) for c in counts]
            + [pltpu.VMEM((2, block, 128), F32)] * 3,
        ),
        out_shape=jax.ShapeDtypeStruct((rows, width), BF16),
        compiler_params=params(),
        cost_estimate=cost(2 * rows * width * 1024, 12 * rows * width),
        name="slide_finish",
    )(gid, start, pos, tokens, emb, wso, *qs, *sums, *tops, *new)


def shifted(x, axis, size, by):
    return lax.ppermute(x, axis, [(i, (i + by) % size) for i in range(size)])


def gather_shifts(x, axis, size):
    got = [x]
    for k in range(1, size):
        got.append(shifted(x, axis, size, k))
    return got


def after(x, *others):
    return lax.optimization_barrier((x,) + others)[0]


def gather_line(x, axis, size, place, gate, pick=True):
    if size != 4:
        got = gather_shifts(x, axis, size)
        return got if pick else got[:1] + [(g, g) for g in got[1:]]
    right = lax.ppermute(x, axis, [(0, 1), (1, 2), (2, 3)])
    left = lax.ppermute(x, axis, [(3, 2), (2, 1), (1, 0)])
    ends, pass_right, pass_left = x, right, left
    if gate:
        ends, pass_right, pass_left = lax.optimization_barrier((x, right, left) + tuple(gate))[:3]
    right_two = lax.ppermute(pass_right, axis, [(1, 2), (2, 3)])
    left_two = lax.ppermute(pass_left, axis, [(2, 1), (1, 0)])
    across = lax.ppermute(ends, axis, [(0, 3), (3, 0)])
    pairs = [(right, across), (right_two, left_two), (across, left)]
    if not pick:
        return [x] + pairs
    return [x] + [jnp.where(place >= k, *pair) for k, pair in enumerate(pairs, 1)]


def swapped(x, axis, size, bit):
    return lax.ppermute(x, axis, [(i, i ^ bit) for i in range(size)])


def shards(
    tile_patches,
    w_patch,
    w_tqkv,
    w_to,
    w_gu,
    w_down,
    tile_gain,
    w_in,
    slide_tokens,
    slide_gain,
    w_sqkv,
    w_so,
    pattern_of_group,
    new_positions,
):
    devs = lax.axis_size("dev")
    grps = lax.axis_size("grp")
    dev = lax.axis_index("dev")
    grp = lax.axis_index("grp")
    rows, width = slide_tokens.shape
    place = grp * devs + dev
    ratios = (1, devs, devs * grps // 4, devs * grps)
    counts = [rows // r for r in ratios]
    group_width = width // GROUPS
    news = new_positions.shape[0]

    ring_dev = lax.rem(dev - lax.iota(jnp.int32, devs) + devs, devs)

    patches = gather_shifts(tile_patches, "dev", devs)

    gid = jnp.sum(
        jnp.where(
            pattern_of_group[None, :] == lax.iota(jnp.int32, 4)[:, None], lax.iota(jnp.int32, GROUPS)[None, :], 0
        ),
        axis=1,
    ).astype(jnp.int32)
    gain_row = slide_gain.reshape(1, width)
    q0, q1, q2, q3, kv0, kv_near, kv_far, w_slide = slide_proj(gid, slide_tokens, gain_row, w_sqkv, ratios)
    qs = [q0, q1, q2, q3]

    pieces = grps
    while (w_to.shape[0] // pieces) % 16:
        pieces //= 2
    piece_rows = w_to.shape[0] // pieces
    mine = lax.dynamic_slice_in_dim(w_to, lax.rem(grp, pieces) * piece_rows, piece_rows, 0)
    far_rows = kv_far.shape[0]
    chunks = kv_far.shape[1] // (2 * USED)
    together = pieces == grps and kv_far.shape[1] == w_to.shape[1]
    bits = [1 << b for b in range(grps.bit_length() - 1)]
    bits = bits[1:] + bits[:1]

    def plane(x, count):
        held, tags = [jnp.stack(gather_shifts(x, "dev", devs))], [0]
        for bit in bits:
            if bit < count:
                held = held + [swapped(h, "grp", grps, bit) for h in held]
                tags = tags + [t ^ bit for t in tags]
        return held, tags

    if together:
        far, tags = plane(jnp.concatenate([mine, kv_far], axis=0), grps)
        lasts, sources, last_row = far, tags, piece_rows
    else:
        far, tags = plane(mine, pieces)
        lasts, sources = plane(kv_far, grps)
        last_row = 0
    order = jnp.bitwise_xor(lax.rem(grp, pieces), jnp.array(tags, jnp.int32))
    order = jnp.concatenate([order, dev[None]])

    x0, att = tile_front(ring_dev, patches, w_patch, w_tqkv, tile_gain)
    atts = gather_line(att, "dev", devs, dev, (), pick=False)
    arrived = [a for pair in atts[1:] for a in pair]

    kv_near = after(kv_near, *patches)
    shipped = gather_line(kv_near, "dev", devs, dev, tuple(arrived))
    tails = [jnp.stack([x[counts[1] :] for x in shipped])]
    near_sources = [0]
    near = grps // 4
    for bit in [1 << b for b in range(near.bit_length() - 1)]:
        tails = tails + [swapped(t, "grp", grps, bit) for t in tails]
        near_sources = near_sources + [t ^ bit for t in near_sources]
    kvs = [
        ([kv0], [0], [((0, rows), 0)]),
        (shipped, list(range(devs)), [((0, counts[1]), 0)] * devs),
        (
            tails,
            [t for t in range(len(tails)) for _ in range(devs)],
            [(k, (0, counts[2]), 0) for _ in tails for k in range(devs)],
        ),
        (
            lasts,
            [t for t in range(len(lasts)) for _ in range(devs * chunks)],
            [
                (k, (last_row, last_row + far_rows), c * 2 * USED)
                for _ in lasts
                for k in range(devs)
                for c in range(chunks)
            ],
        ),
    ]

    def devices_of(tags):
        return (jnp.bitwise_xor(grp, jnp.array(tags, jnp.int32))[:, None] * devs + ring_dev[None]).reshape(-1)

    blocks = [place[None], devices_of([0]), devices_of(near_sources), devices_of(sources)]
    at = jnp.stack(
        [
            (blocks[p][:, None] * rows + lax.iota(jnp.int32, counts[p])[None] * ratios[p]).reshape(1, rows)
            for p in range(4)
        ]
    )
    at = after(at, *patches)

    block = slide_block(rows, ratios)
    first_half = slide_attend(new_positions, at[0], after(q0, att), kvs[0], 1, block, 0)
    states = [slide_attend(new_positions, at[0], q0, kvs[0], 1, block, 1, first_half)]
    x0 = after(x0, *states[0])
    for p in range(1, 4):
        states.append(slide_attend(new_positions, at[p], qs[p], kvs[p], ratios[p], block // ratios[p]))
    sums = [a for a, _ in states]
    tops = [b for _, b in states]

    pooled = tile_back(x0, atts, w_to, far, w_gu, w_down, tile_gain, order)
    parts = jnp.stack(gather_shifts(pooled[0], "dev", devs))
    tiles = x0.shape[0] // PATCHES
    tile_embed = embed(ring_dev, parts, pooled[1], tile_gain, w_in, tiles)
    every = [tile_embed]
    tags = [0]
    for bit in bits:
        every = every + [swapped(e, "grp", grps, bit) for e in every]
        tags = tags + [t ^ bit for t in tags]
    every = jnp.concatenate(every, axis=0)
    owners = jnp.bitwise_xor(grp, jnp.array(tags, jnp.int32))
    new_here = new_positions.reshape(grps, tiles)[owners].reshape(news)

    slots = -(-news // 16) * 16
    padded = jnp.pad(every, ((0, slots - news), (0, 0))).astype(F32)
    pos_column = jnp.pad(new_here, (0, slots - news)).reshape(slots, 1)
    seg = jnp.stack([place * rows, jnp.int32(rows)]).astype(jnp.int32)
    new = fresh(seg, gid, new_positions, padded, pos_column, gain_row, w_slide, at, kvs, ratios)
    start = (place * rows).reshape(1).astype(jnp.int32)
    slide_out = finish(
        gid,
        start,
        new_here,
        slide_tokens,
        padded,
        w_so.reshape(GROUPS, group_width, width),
        qs,
        sums,
        tops,
        new,
        ratios,
        news,
    )
    return (tile_embed, slide_out)


def solution(mesh):
    placed = (
        P(("grp", "dev"), None),
        P(),
        P(None, None, "dev"),
        P("dev", None),
        P(None, None, "dev"),
        P("dev", None),
        P(),
        P(),
        P(("grp", "dev"), None),
        P(),
        P(),
        P(),
        P(),
        P(),
    )

    return jax.shard_map(
        shards,
        mesh=mesh,
        in_specs=placed,
        out_specs=(P("grp", None), P(("grp", "dev"), None)),
        check_vma=False,
    )
```

profile of v0, /device:TPU:0, one launch (start us, length us, event | category | flops | bytes accessed | tf_op | source)
XLA Modules:
  0.0 230.2 jit_solution(1159667959357737851)
XLA Ops:
  0.6 3.1 %collective-permute-start = (bf16[192,588]{1,0:T(8,128)(2,1)}, bf16[192,588]{1,0:T(8,128)(2,1)S(1)}, u32[]{:S(2)}, u32[]{:S(2)}) collective-permute-start(bf16[192,588]{1,0:T(8,128)(2,1)} %rest_0_.1), channel_id=1, source_target_pairs={{0,1},{1,2},{2,3},{3,0},{4,5},{5,6},{6,7},{7,4},{8,9},{9,10},{10,1... | collective-permute-start | bytes 677384 | tf_op jit(solution)/shard_map/ppermute | solution.py:682
  3.7 2.6 %collective-permute-start.1 = (bf16[192,588]{1,0:T(8,128)(2,1)}, bf16[192,588]{1,0:T(8,128)(2,1)S(1)}, u32[]{:S(2)}, u32[]{:S(2)}) collective-permute-start(bf16[192,588]{1,0:T(8,128)(2,1)} %rest_0_.1), channel_id=1, source_target_pairs={{0,2},{1,3},{2,0},{3,1},{4,6},{5,7},{6,4},{7,5},{8,10},{9,11},{10,... | collective-permute-start | bytes 677384 | tf_op jit(solution)/shard_map/ppermute | solution.py:682
  11.2 15.2 %slide_proj.1 = (bf16[2048,256]{1,0:T(8,128)(2,1)}, bf16[512,256]{1,0:T(8,128)(2,1)}, bf16[256,256]{1,0:T(8,128)(2,1)}, bf16[64,256]{1,0:T(8,128)(2,1)}, bf16[20...) custom-call(s32[4]{0:T(128)} %select_reduce_fusion.gid_ref, ...), custom_call_target="tpu_custom_call" | custom-call | flops 5234491392 | bytes 12976128 | tf_op jit(solution)/shard_map/slide_proj/pallas_call | solution.py:318
  33.7 13.9 %tile_front.1 = (bf16[768,1536]{1,0:T(8,128)(2,1)}, bf16[768,384]{1,0:T(8,128)(2,1)}) custom-call(s32[4]{0:T(128)} %copy-done.19, bf16[192,588]{1,0:T(8,128)(2,1)} %rest_0_.1, bf16[192,588]{1,0:T(8,128)(2,1)} %copy-done.24, bf16[192,588]{1,0:T(8,128)(2,1)} %copy-done.25, bf16[192,588]{1,0:T(8,128)(2,1)} %copy-done.26, bf16[588,1536]{1,0:T(8,128)(2,1)} %rest_4_.1, ...), custom_call_target="tpu_custom_call" | custom-call | flops 4105175040 | bytes 9197568 | tf_op jit(solution)/shard_map/tile_front/pallas_call | solution.py:91
  47.5 3.6 %collective-permute-start.3 = (bf16[768,384]{1,0:T(8,128)(2,1)}, bf16[768,384]{1,0:T(8,128)(2,1)S(1)}, u32[]{:S(2)}, u32[]{:S(2)}) collective-permute-start(bf16[768,384]{1,0:T(8,128)(2,1)} %get-tuple-element.38.rest_0_), channel_id=1, source_target_pairs={{0,1},{1,2},{2,3},{4,5},{5,6},{6,7},{8,9},{9,10},{10,11},{12,13},{... | collective-permute-start | bytes 1769480 | tf_op jit(solution)/shard_map/ppermute | solution.py:700
  51.2 3.3 %collective-permute-start.4 = (bf16[768,384]{1,0:T(8,128)(2,1)}, bf16[768,384]{1,0:T(8,128)(2,1)}, u32[]{:S(2)}, u32[]{:S(2)}) collective-permute-start(bf16[768,384]{1,0:T(8,128)(2,1)} %get-tuple-element.38.rest_0_), channel_id=1, source_target_pairs={{0,3},{3,0},{4,7},{7,4},{8,11},{11,8},{12,15},{15,12},{16,19},{19,... | collective-permute-start | bytes 1769480 | tf_op jit(solution)/shard_map/ppermute | solution.py:707
  57.5 4.6 %collective-permute-start.28 = (bf16[768,384]{1,0:T(8,128)(2,1)S(1)}, bf16[768,384]{1,0:T(8,128)(2,1)S(1)}, u32[]{:S(2)}, u32[]{:S(2)}) collective-permute-start(bf16[768,384]{1,0:T(8,128)(2,1)S(1)} %copy-done.9), channel_id=1, source_target_pairs={{0,1},{1,2},{2,3},{4,5},{5,6},{6,7},{8,9},{9,10},{10,11},{12,13},{... | collective-permute-start | bytes 1769480 | tf_op jit(solution)/shard_map/ppermute | solution.py:700
  62.7 2.4 %collective-permute-done.3.rest_1_ = bf16[768,384]{1,0:T(8,128)(2,1)S(1)} collective-permute-done((bf16[768,384]{1,0:T(8,128)(2,1)}, bf16[768,384]{1,0:T(8,128)(2,1)S(1)}, u32[]{:S(2)}, u32[]{:S(2)}) %collective-permute-start.3) | collective-permute-done | bytes 589856 | tf_op jit(solution)/shard_map/ppermute | solution.py:700
  66.4 11.4 %collective-permute-done.4.rest_2_.rest_5_ = bf16[768,384]{1,0:T(8,128)(2,1)} collective-permute-done((bf16[768,384]{1,0:T(8,128)(2,1)}, bf16[768,384]{1,0:T(8,128)(2,1)}, u32[]{:S(2)}, u32[]{:S(2)}) %collective-permute-start.4) | collective-permute-done | bytes 589856 | tf_op jit(solution)/shard_map/ppermute | solution.py:707
  79.3 1.8 collective-permute-done.6.rest_6_
  82.4 13.7 %shard_map.194 = (f32[2048,256]{1,0:T(8,128)}, f32[4,64,512]{2,1,0:T(8,128)}) custom-call(s32[24]{0:T(128)} %news_ref.1, s32[1,2048]{1,0:T(1,128)} %get-tuple-element.76.at_ref, bf16[2048,256]{1,0:T(8,128)(2,1)} %get-tuple-element.39.q_ref.rest_0_, bf16[2048,384]{1,0:T(8,128)(2,1)} %get-tuple-element.37.rest_0_), custom_call_target="tpu_custom_call" | custom-call | flops 8589934592 | bytes 3145728 | tf_op jit(solution)/shard_map/pallas_call | solution.py:460
  98.3 8.0 %collective-permute-done.7.rest_4_ = bf16[768,384]{1,0:T(8,128)(2,1)} collective-permute-done((bf16[768,384]{1,0:T(8,128)(2,1)}, bf16[768,384]{1,0:T(8,128)(2,1)}, u32[]{:S(2)}, u32[]{:S(2)}) %collective-permute-start.7) | collective-permute-done | bytes 589856 | tf_op jit(solution)/shard_map/ppermute | solution.py:706
  109.2 13.7 %shard_map.195 = (f32[2048,256]{1,0:T(8,128)}, f32[4,64,512]{2,1,0:T(8,128)}) custom-call(s32[24]{0:T(128)} %news_ref.1, s32[1,2048]{1,0:T(1,128)} %get-tuple-element.76.at_ref, bf16[2048,256]{1,0:T(8,128)(2,1)} %get-tuple-element.39.q_ref.rest_0_, bf16[2048,384]{1,0:T(8,128)(2,1)} %get-tuple-element.37.rest_0_, ...), custom_call_target="tpu_custom_call", output_to_operand_aliasing={{0}: (4, {}), {1}: (5, {})} | custom-call | flops 8589934592 | bytes 3145728 | tf_op jit(solution)/shard_map/pallas_call | solution.py:460
  123.0 1.9 collective-permute-start.30
  125.1 7.5 %collective-permute-done.13.rest_10_.rest_3_ = bf16[4,64,1536]{2,1,0:T(8,128)(2,1)} collective-permute-done((bf16[4,64,1536]{2,1,0:T(8,128)(2,1)S(1)}, bf16[4,64,1536]{2,1,0:T(8,128)(2,1)}, u32[]{:S(2)}, u32[]{:S(2)}) %collective-permute-start.13) | collective-permute-done | bytes 786464 | tf_op jit(solution)/shard_map/ppermute | solution.py:715
  134.3 6.2 %collective-permute-done.30 = bf16[768,384]{1,0:T(8,128)(2,1)S(1)} collective-permute-done((bf16[768,384]{1,0:T(8,128)(2,1)S(1)}, bf16[768,384]{1,0:T(8,128)(2,1)S(1)}, u32[]{:S(2)}, u32[]{:S(2)}) %collective-permute-start.30) | collective-permute-done | bytes 589856 | tf_op jit(solution)/shard_map/ppermute | solution.py:707
  144.2 18.1 %tile_back.1 = f32[2,8,1536]{2,1,0:T(8,128)} custom-call(bf16[768,1536]{1,0:T(8,128)(2,1)} %get-tuple-element.44.x0_ref, bf16[768,384]{1,0:T(8,128)(2,1)} %get-tuple-element.38.rest_0_, bf16[768,384]{1,0:T(8,128)(2,1)} %copy-done.23, bf16[768,384]{1,0:T(8,128)(2,1)} %collective-permute-done.4.rest_2_.rest_5_, ...), custom_call_target="tpu_custom_call" | custom-call | flops 8455716864 | bytes 18874368 | tf_op jit(solution)/shard_map/tile_back/pallas_call | solution.py:189
  166.1 1.8 collective-permute-done.20
  171.5 3.0 %tile_embed.1 = bf16[3,768]{1,0:T(4,128)(2,1)} custom-call(s32[4]{0:T(128)} %copy-done.19, f32[4,8,1536]{2,1,0:T(8,128)} %pad_maximum_fusion.3.parts_ref, f32[8,1536]{1,0:T(8,128)} %get-tuple-element.70.mean_ref, f32[3,1536]{1,0:T(4,128)} %gain_ref.1, bf16[1536,768]{1,0:T(8,128)(2,1)} %win_ref.1), custom_call_target="tpu_custom_call" | custom-call | flops 18874368 | bytes 2359296 | tf_op jit(solution)/shard_map/tile_embed/pallas_call | solution.py:220
  179.9 8.3 %shard_map.196 = (f32[512,256]{1,0:T(8,128)}, f32[4,64,128]{2,1,0:T(8,128)}) custom-call(s32[24]{0:T(128)} %news_ref.1, s32[1,2048]{1,0:T(1,128)} %get-tuple-element.75.at_ref, bf16[512,256]{1,0:T(8,128)(2,1)} %get-tuple-element.46.q_ref.rest_1_, bf16[768,384]{1,0:T(8,128)(2,1)} %get-tuple-element.51.rest_0_.rest_1_, bf16[768,384]{1,0:T(8,128)(2,1)} %copy-done.3, ...), custom_call_target="tpu_custom_call" | custom-call | flops 4294967296 | bytes 2359296 | tf_op jit(solution)/shard_map/pallas_call | solution.py:460
  189.3 5.2 %shard_map.198 = (f32[64,256]{1,0:T(8,128)}, f32[4,64,16]{2,1,0:T(8,128)}) custom-call(s32[24]{0:T(128)} %news_ref.1, s32[1,2048]{1,0:T(1,128)} %get-tuple-element.73.at_ref, bf16[64,256]{1,0:T(8,128)(2,1)} %get-tuple-element.48.q_ref.rest_3_, bf16[4,64,1536]{2,1,0:T(8,128)(2,1)} %copy-done, bf16[4,64,1536]{2,1,0:T(8,128)(2,1)} %copy-done.4, ...), custom_call_target="tpu_custom_call" | custom-call | flops 536870912 | bytes 1671168 | tf_op jit(solution)/shard_map/pallas_call | solution.py:460
  196.6 5.2 %shard_map.197 = (f32[256,256]{1,0:T(8,128)}, f32[4,64,64]{2,1,0:T(8,128)}) custom-call(s32[24]{0:T(128)} %news_ref.1, s32[1,2048]{1,0:T(1,128)} %get-tuple-element.74.at_ref, bf16[256,256]{1,0:T(8,128)(2,1)} %get-tuple-element.47.q_ref.rest_2_, bf16[4,256,384]{2,1,0:T(8,128)(2,1)} %copy-done.8, bf16[4,256,384]{2,1,0:T(8,128)(2,1)} %copy-done.10), custom_call_target="tpu_custom_call" | custom-call | flops 2147483648 | bytes 1966080 | tf_op jit(solution)/shard_map/pallas_call | solution.py:460
  201.8 11.1 %slide_fresh.1 = (f32[4,32,256]{2,1,0:T(8,128)}, f32[4,32,256]{2,1,0:T(8,128)}, f32[4,64,32]{2,1,0:T(8,128)}, bf16[4,128,256]{2,1,0:T(8,128)(2,1)}, bf16[4,128,256]{2,1,0:T(8,128)(2,1)}) custom-call(s32[2]{0:T(128)} %pad_add_fusion.2.seg_ref, s32[4]{0:T(128)} %select_reduce_fusion.gid_ref, s32[24]{0:T(128)} %news_ref.1, f32[32,768]{1,0:T(8,128)} %pad_convert_fusion.emb_ref, ...), custom_call_target="tpu_custom_call" | custom-call | flops 1073741824 | bytes 10223616 | tf_op jit(solution)/shard_map/slide_fresh/pallas_call | solution.py:529
  212.9 17.1 %slide_finish.1 = bf16[2048,768]{1,0:T(8,128)(2,1)} custom-call(s32[4]{0:T(128)} %select_reduce_fusion.gid_ref, s32[1]{0:T(128)} %bitcast.11.start_ref, s32[24]{0:T(128)} %copy-done.20, bf16[2048,768]{1,0:T(8,128)(2,1)} %x_ref.3, f32[32,768]{1,0:T(8,128)} %pad_convert_fusion.emb_ref, bf16[4,192,768]{2,1,0:T(8,128)(2,1)} %bitcast.33, ...), custom_call_target="tpu_custom_call" | custom-call | flops 3221225472 | bytes 18874368 | tf_op jit(solution)/shard_map/slide_finish/pallas_call | solution.py:657
  (152 shorter events, 45.9 us)
Async XLA Ops:
  0.6 31.5 %collective-permute-start = (bf16[192,588]{1,0:T(8,128)(2,1)}, bf16[192,588]{1,0:T(8,128)(2,1)S(1)}, u32[]{:S(2)}, u32[]{:S(2)}) collective-permute-start(bf16[192,588]{1,0:T(8,128)(2,1)} %rest_0_.1), channel_id=1, source_target_pairs={{0,1},{1,2},{2,3},{3,0},{4,5},{5,6},{6,7},{7,4},{8,9},{9,10},{10,1... | collective-permute-start | bytes 677384 | tf_op jit(solution)/shard_map/ppermute | solution.py:682
  3.7 28.5 %collective-permute-start.1 = (bf16[192,588]{1,0:T(8,128)(2,1)}, bf16[192,588]{1,0:T(8,128)(2,1)S(1)}, u32[]{:S(2)}, u32[]{:S(2)}) collective-permute-start(bf16[192,588]{1,0:T(8,128)(2,1)} %rest_0_.1), channel_id=1, source_target_pairs={{0,2},{1,3},{2,0},{3,1},{4,6},{5,7},{6,4},{7,5},{8,10},{9,11},{10,... | collective-permute-start | bytes 677384 | tf_op jit(solution)/shard_map/ppermute | solution.py:682
  6.3 25.9 %collective-permute-start.2 = (bf16[192,588]{1,0:T(8,128)(2,1)}, bf16[192,588]{1,0:T(8,128)(2,1)S(1)}, u32[]{:S(2)}, u32[]{:S(2)}) collective-permute-start(bf16[192,588]{1,0:T(8,128)(2,1)} %rest_0_.1), channel_id=1, source_target_pairs={{0,3},{1,0},{2,1},{3,2},{4,7},{5,4},{6,5},{7,6},{8,11},{9,8},{10,9... | collective-permute-start | bytes 677384 | tf_op jit(solution)/shard_map/ppermute | solution.py:682
  27.2 27.3 %collective-permute-start.10 = (bf16[64,1536]{1,0:T(8,128)(2,1)S(1)}, bf16[64,1536]{1,0:T(8,128)(2,1)S(1)}, u32[]{:S(2)}, u32[]{:S(2)}) collective-permute-start(bf16[64,1536]{1,0:T(8,128)(2,1)S(1)} %get-tuple-element.69), channel_id=1, source_target_pairs={{0,3},{1,0},{2,1},{3,2},{4,7},{5,4},{6,5},{7,6},{8,11},{9,8},{10,9... | collective-permute-start | bytes 589832 | tf_op jit(solution)/shard_map/ppermute | solution.py:682
  27.7 28.1 %collective-permute-start.9 = (bf16[64,1536]{1,0:T(8,128)(2,1)S(1)}, bf16[64,1536]{1,0:T(8,128)(2,1)S(1)}, u32[]{:S(2)}, u32[]{:S(2)}) collective-permute-start(bf16[64,1536]{1,0:T(8,128)(2,1)S(1)} %get-tuple-element.69), channel_id=1, source_target_pairs={{0,2},{1,3},{2,0},{3,1},{4,6},{5,7},{6,4},{7,5},{8,10},{9,11},{10,... | collective-permute-start | bytes 589832 | tf_op jit(solution)/shard_map/ppermute | solution.py:682
  32.1 23.7 %collective-permute-start.8 = (bf16[64,1536]{1,0:T(8,128)(2,1)S(1)}, bf16[64,1536]{1,0:T(8,128)(2,1)S(1)}, u32[]{:S(2)}, u32[]{:S(2)}) collective-permute-start(bf16[64,1536]{1,0:T(8,128)(2,1)S(1)} %get-tuple-element.69), channel_id=1, source_target_pairs={{0,1},{1,2},{2,3},{3,0},{4,5},{5,6},{6,7},{7,4},{8,9},{9,10},{10,1... | collective-permute-start | bytes 589832 | tf_op jit(solution)/shard_map/ppermute | solution.py:682
  47.5 17.6 %collective-permute-start.3 = (bf16[768,384]{1,0:T(8,128)(2,1)}, bf16[768,384]{1,0:T(8,128)(2,1)S(1)}, u32[]{:S(2)}, u32[]{:S(2)}) collective-permute-start(bf16[768,384]{1,0:T(8,128)(2,1)} %get-tuple-element.38.rest_0_), channel_id=1, source_target_pairs={{0,1},{1,2},{2,3},{4,5},{5,6},{6,7},{8,9},{9,10},{10,11},{12,13},{... | collective-permute-start | bytes 1769480 | tf_op jit(solution)/shard_map/ppermute | solution.py:700
  51.2 26.7 %collective-permute-start.4 = (bf16[768,384]{1,0:T(8,128)(2,1)}, bf16[768,384]{1,0:T(8,128)(2,1)}, u32[]{:S(2)}, u32[]{:S(2)}) collective-permute-start(bf16[768,384]{1,0:T(8,128)(2,1)} %get-tuple-element.38.rest_0_), channel_id=1, source_target_pairs={{0,3},{3,0},{4,7},{7,4},{8,11},{11,8},{12,15},{15,12},{16,19},{19,... | collective-permute-start | bytes 1769480 | tf_op jit(solution)/shard_map/ppermute | solution.py:707
  54.5 26.6 %collective-permute-start.6 = (bf16[768,384]{1,0:T(8,128)(2,1)}, bf16[768,384]{1,0:T(8,128)(2,1)}, u32[]{:S(2)}, u32[]{:S(2)}) collective-permute-start(bf16[768,384]{1,0:T(8,128)(2,1)} %get-tuple-element.38.rest_0_), channel_id=1, source_target_pairs={{3,2},{2,1},{1,0},{7,6},{6,5},{5,4},{11,10},{10,9},{9,8},{15,14},{... | collective-permute-start | bytes 1769480 | tf_op jit(solution)/shard_map/ppermute | solution.py:701
  55.9 41.8 %collective-permute-start.11 = (bf16[4,64,1536]{2,1,0:T(8,128)(2,1)S(1)}, bf16[4,64,1536]{2,1,0:T(8,128)(2,1)S(1)}, u32[]{:S(2)}, u32[]{:S(2)}) collective-permute-start(bf16[4,64,1536]{2,1,0:T(8,128)(2,1)S(1)} %pad_maximum_fusion.rest_7_.rest_0_), channel_id=1, source_target_pairs={{0,8},{4,12},{8,0},{12,4},{16,24},{20,28},{24,16},{28,20},{1,9},{5... | collective-permute-start | bytes 2359304 | tf_op jit(solution)/shard_map/ppermute | solution.py:715
  57.5 38.6 %collective-permute-start.28 = (bf16[768,384]{1,0:T(8,128)(2,1)S(1)}, bf16[768,384]{1,0:T(8,128)(2,1)S(1)}, u32[]{:S(2)}, u32[]{:S(2)}) collective-permute-start(bf16[768,384]{1,0:T(8,128)(2,1)S(1)} %copy-done.9), channel_id=1, source_target_pairs={{0,1},{1,2},{2,3},{4,5},{5,6},{6,7},{8,9},{9,10},{10,11},{12,13},{... | collective-permute-start | bytes 1769480 | tf_op jit(solution)/shard_map/ppermute | solution.py:700
  65.2 33.1 %collective-permute-start.29 = (bf16[768,384]{1,0:T(8,128)(2,1)S(1)}, bf16[768,384]{1,0:T(8,128)(2,1)S(1)}, u32[]{:S(2)}, u32[]{:S(2)}) collective-permute-start(bf16[768,384]{1,0:T(8,128)(2,1)S(1)} %copy-done.9), channel_id=1, source_target_pairs={{3,2},{2,1},{1,0},{7,6},{6,5},{5,4},{11,10},{10,9},{9,8},{15,14},{... | collective-permute-start | bytes 1769480 | tf_op jit(solution)/shard_map/ppermute | solution.py:701
  77.8 20.4 %collective-permute-start.5 = (bf16[768,384]{1,0:T(8,128)(2,1)S(1)}, bf16[768,384]{1,0:T(8,128)(2,1)}, u32[]{:S(2)}, u32[]{:S(2)}) collective-permute-start(bf16[768,384]{1,0:T(8,128)(2,1)S(1)} %collective-permute-done.3.rest_1_), channel_id=1, source_target_pairs={{1,2},{2,3},{5,6},{6,7},{9,10},{10,11},{13,14},{14,15},{17,18},{18... | collective-permute-start | bytes 1769480 | tf_op jit(solution)/shard_map/ppermute | solution.py:705
  81.1 25.2 %collective-permute-start.7 = (bf16[768,384]{1,0:T(8,128)(2,1)}, bf16[768,384]{1,0:T(8,128)(2,1)}, u32[]{:S(2)}, u32[]{:S(2)}) collective-permute-start(bf16[768,384]{1,0:T(8,128)(2,1)} %collective-permute-done.6.rest_6_), channel_id=1, source_target_pairs={{2,1},{1,0},{6,5},{5,4},{10,9},{9,8},{14,13},{13,12},{18,17},{17,1... | collective-permute-start | bytes 1769480 | tf_op jit(solution)/shard_map/ppermute | solution.py:706
  96.2 28.8 %collective-permute-start.12 = (bf16[4,64,1536]{2,1,0:T(8,128)(2,1)S(1)}, bf16[4,64,1536]{2,1,0:T(8,128)(2,1)}, u32[]{:S(2)}, u32[]{:S(2)}) collective-permute-start(bf16[4,64,1536]{2,1,0:T(8,128)(2,1)S(1)} %pad_maximum_fusion.rest_7_.rest_0_), channel_id=1, source_target_pairs={{0,16},{4,20},{8,24},{12,28},{16,0},{20,4},{24,8},{28,12},{1,17},{... | collective-permute-start | bytes 2359304 | tf_op jit(solution)/shard_map/ppermute | solution.py:715
  97.7 34.8 %collective-permute-start.13 = (bf16[4,64,1536]{2,1,0:T(8,128)(2,1)S(1)}, bf16[4,64,1536]{2,1,0:T(8,128)(2,1)}, u32[]{:S(2)}, u32[]{:S(2)}) collective-permute-start(bf16[4,64,1536]{2,1,0:T(8,128)(2,1)S(1)} %collective-permute-done.11.rest_8_.rest_1_), channel_id=1, source_target_pairs={{0,16},{4,20},{8,24},{12,28},{16,0},{20,4},{24,8},{28,12},{1,17},{... | collective-permute-start | bytes 2359304 | tf_op jit(solution)/shard_map/ppermute | solution.py:715
  106.3 26.3 %collective-permute-start.31 = (bf16[768,384]{1,0:T(8,128)(2,1)S(1)}, bf16[768,384]{1,0:T(8,128)(2,1)}, u32[]{:S(2)}, u32[]{:S(2)}) collective-permute-start(bf16[768,384]{1,0:T(8,128)(2,1)S(1)} %collective-permute-done.28), channel_id=1, source_target_pairs={{1,2},{2,3},{5,6},{6,7},{9,10},{10,11},{13,14},{14,15},{17,18},{18... | collective-permute-start | bytes 1769480 | tf_op jit(solution)/shard_map/ppermute | solution.py:705
  107.8 25.3 %collective-permute-start.32 = (bf16[768,384]{1,0:T(8,128)(2,1)S(1)}, bf16[768,384]{1,0:T(8,128)(2,1)}, u32[]{:S(2)}, u32[]{:S(2)}) collective-permute-start(bf16[768,384]{1,0:T(8,128)(2,1)S(1)} %collective-permute-done.29), channel_id=1, source_target_pairs={{2,1},{1,0},{6,5},{5,4},{10,9},{9,8},{14,13},{13,12},{18,17},{17,1... | collective-permute-start | bytes 1769480 | tf_op jit(solution)/shard_map/ppermute | solution.py:706
  123.0 17.6 %collective-permute-start.30 = (bf16[768,384]{1,0:T(8,128)(2,1)S(1)}, bf16[768,384]{1,0:T(8,128)(2,1)S(1)}, u32[]{:S(2)}, u32[]{:S(2)}) collective-permute-start(bf16[768,384]{1,0:T(8,128)(2,1)S(1)} %copy-done.9), channel_id=1, source_target_pairs={{0,3},{3,0},{4,7},{7,4},{8,11},{11,8},{12,15},{15,12},{16,19},{19,... | collective-permute-start | bytes 1769480 | tf_op jit(solution)/shard_map/ppermute | solution.py:707
  125.0 16.5 %collective-permute-start.14 = (bf16[4,64,1536]{2,1,0:T(8,128)(2,1)S(1)}, bf16[4,64,1536]{2,1,0:T(8,128)(2,1)S(1)}, u32[]{:S(2)}, u32[]{:S(2)}) collective-permute-start(bf16[4,64,1536]{2,1,0:T(8,128)(2,1)S(1)} %pad_maximum_fusion.rest_7_.rest_0_), channel_id=1, source_target_pairs={{0,4},{4,0},{8,12},{12,8},{16,20},{20,16},{24,28},{28,24},{1,5},{5... | collective-permute-start | bytes 2359304 | tf_op jit(solution)/shard_map/ppermute | solution.py:715
  133.1 11.2 %collective-permute-start.17 = (bf16[4,64,1536]{2,1,0:T(8,128)(2,1)}, bf16[4,64,1536]{2,1,0:T(8,128)(2,1)}, u32[]{:S(2)}, u32[]{:S(2)}) collective-permute-start(bf16[4,64,1536]{2,1,0:T(8,128)(2,1)} %collective-permute-done.13.rest_10_.rest_3_), channel_id=1, source_target_pairs={{0,4},{4,0},{8,12},{12,8},{16,20},{20,16},{24,28},{28,24},{1,5},{5... | collective-permute-start | bytes 2359304 | tf_op jit(solution)/shard_map/ppermute | solution.py:715
  166.0 29.7 %collective-permute-start.33 = (bf16[4,256,384]{2,1,0:T(8,128)(2,1)S(1)}, bf16[4,256,384]{2,1,0:T(8,128)(2,1)S(1)}, u32[]{:S(2)}, u32[]{:S(2)}) collective-permute-start(bf16[4,256,384]{2,1,0:T(8,128)(2,1)S(1)} %pad_maximum_fusion.1.rest_0_.rest_5_), channel_id=1, source_target_pairs={{0,4},{4,0},{8,12},{12,8},{16,20},{20,16},{24,28},{28,24},{1,5},{5... | collective-permute-start | bytes 2359304 | tf_op jit(solution)/shard_map/ppermute | solution.py:715
  177.3 11.5 %collective-permute-start.22 = (bf16[3,768]{1,0:T(4,128)(2,1)}, bf16[3,768]{1,0:T(4,128)(2,1)S(1)}, u32[]{:S(2)}, u32[]{:S(2)}) collective-permute-start(bf16[3,768]{1,0:T(4,128)(2,1)} %tile_embed.1), channel_id=1, source_target_pairs={{0,16},{4,20},{8,24},{12,28},{16,0},{20,4},{24,8},{28,12},{1,17},{... | collective-permute-start | bytes 13832 | tf_op jit(solution)/shard_map/ppermute | solution.py:715
  178.8 10.0 %collective-permute-start.23 = (bf16[3,768]{1,0:T(4,128)(2,1)S(1)}, bf16[3,768]{1,0:T(4,128)(2,1)S(1)}, u32[]{:S(2)}, u32[]{:S(2)}) collective-permute-start(bf16[3,768]{1,0:T(4,128)(2,1)S(1)} %collective-permute-done.21), channel_id=1, source_target_pairs={{0,16},{4,20},{8,24},{12,28},{16,0},{20,4},{24,8},{28,12},{1,17},{... | collective-permute-start | bytes 13832 | tf_op jit(solution)/shard_map/ppermute | solution.py:715
  (37 other events, 520.2 us)
where the time goes:
time: 231 us; the launch traced here: 230 us
  Pallas kernels  125 us (54%)
  starting transfers between devices  42.6 us (18%)
  waiting for transfers between devices  42.1 us (18%)
  local copies, waits for them, and re-layouts  13 us (6%)
  other arithmetic  6.51 us (3%)
    pallas_call x5, Pallas kernels, slide_attend(): pl.pallas_call(functools.partial(slide_attend_kernel, ratio, pos.shape[0]...  46.2 us
    pallas_call x1, Pallas kernels, tile_back(): pl.pallas_call(functools.partial(tile_back_kernel, devs, pieces), grid=(t...  18.1 us
    ppermute x2, waiting for transfers between devices, gather_line(): across = lax.ppermute(ends, axis, [(0, 3), (3, 0)])  17.6 us
    pallas_call x1, Pallas kernels, finish(): pl.pallas_call(functools.partial(finish_kernel, ratios, news), grid_spec=...  17.1 us
    pallas_call x1, Pallas kernels, slide_proj(): pl.pallas_call(functools.partial(slide_proj_kernel, ratios), grid_spec=pl...  15.2 us
    pallas_call x1, Pallas kernels, tile_front(): pl.pallas_call(functools.partial(tile_front_kernel, devs), grid=(tokens /...  13.9 us
    ppermute x9, starting transfers between devices, shifted(): return lax.ppermute(x, axis, [(i, (i + by) % size) for i in range(size)])  11.4 us
    pallas_call x1, Pallas kernels, fresh(): pl.pallas_call(functools.partial(fresh_kernel, ratios, news_pos.shape[0],...  11.1 us
  transfers between devices with their start and end apart: 34, of which 9 were waited for; matrix products, arithmetic and copies ran while one was open for 6% of the time, Pallas kernels for 32%

commit v1 on v0

--- a/solution.py
+++ b/solution.py
@@ -17,7 +17,6 @@
 LOG2E = math.log2(math.e)
 F32 = jnp.float32
 BF16 = jnp.bfloat16
-VMEM_LIMIT = 60 * 1024 * 1024
 
 
 def norm(x, gain):
@@ -38,8 +37,8 @@
     return lax.broadcasted_iota(jnp.int32, shape, len(shape) - 1)
 
 
-def params(**kw):
-    return pltpu.CompilerParams(vmem_limit_bytes=VMEM_LIMIT, **kw)
+def params(mib=60):
+    return pltpu.CompilerParams(vmem_limit_bytes=mib * 1024 * 1024)
 
 
 def cost(flops, bytes_accessed, trans=0):
@@ -117,7 +116,7 @@
     att_refs = rest[: 2 * devs - 1]
     rest = rest[2 * devs - 1 :]
     far_refs = rest[:pieces]
-    (wto_own, wgu_any, wdown_any, gain_ref, order_ref, out_ref, wto, wgu, wdown, hsum, sems) = rest[pieces:]
+    (wto_own, wgu_any, wdown_any, gain_ref, order_ref, out_ref, mean_ref, wto, wgu, wdown, hsum, sems) = rest[pieces:]
     step = pl.program_id(0)
     rows = wto_own.shape[0]
     piece = rows // pieces
@@ -145,14 +144,17 @@
         gu(1).start()
         down().start()
         hsum[...] = jnp.zeros_like(hsum)
-        out_ref[...] = jnp.zeros_like(out_ref)
+        mean_ref[...] = jnp.zeros_like(mean_ref)
         own().wait()
-        for k in range(1, devs):
+
+    x1 = x0_ref[...].astype(F32) + mm(att_refs[0][...], wto[0])
+    for k in range(1, devs):
+
+        @pl.when(step == 0)
+        def _(k=k):
             for b in range(pieces):
                 far(k, b).wait()
 
-    x1 = x0_ref[...].astype(F32) + mm(att_refs[0][...], wto[0])
-    for k in range(1, devs):
         near = order_ref[pieces] >= k
         att = jnp.where(near, att_refs[2 * k - 1][...], att_refs[2 * k][...])
         x1 = x1 + mm(att, wto[k])
@@ -167,15 +169,15 @@
     gate = mm(h2, wgu[0])
     up = mm(h2, wgu[1])
     hidden = (gate * (1.0 / (1.0 + jnp.exp(-gate))) * up).astype(BF16).astype(F32)
-    out_ref[1, pl.ds(step, 1), :] = jnp.mean(x1, axis=0, keepdims=True)
+    mean_ref[pl.ds(step, 1), :] = jnp.mean(x1, axis=0, keepdims=True)
     hsum[pl.ds(step, 1), :] = jnp.mean(hidden, axis=0, keepdims=True)
 
     @pl.when(step == pl.num_programs(0) - 1)
     def _():
         down().wait()
-        high = hsum[...].astype(BF16)
-        low = (hsum[...] - high.astype(F32)).astype(BF16)
-        out_ref[0] = mm(high, wdown[...]) + mm(low, wdown[...])
+        high = hsum[...].astype(BF16).astype(F32)
+        both = mm(jnp.concatenate([high, hsum[...] - high], axis=0).astype(BF16), wdown[...])
+        out_ref[...] = both[0:8] + both[8:16]
 
 
 def tile_back(x0, atts, wto_own, wto_far, w_gu, w_down, gain, order):
@@ -193,8 +195,8 @@
         + [pl.BlockSpec((PATCHES, part), lambda i: (i, 0))] * (2 * devs - 1)
         + [anyspec] * (pieces + 3)
         + [whole(gain.shape), pl.BlockSpec(memory_space=pltpu.SMEM)],
-        out_specs=whole((2, 8, width)),
-        out_shape=jax.ShapeDtypeStruct((2, 8, width), F32),
+        out_specs=[whole((8, width))] * 2,
+        out_shape=[jax.ShapeDtypeStruct((8, width), F32)] * 2,
         scratch_shapes=[
             pltpu.VMEM((devs, part, width), BF16),
             pltpu.VMEM(w_gu.shape, BF16),
@@ -208,29 +210,41 @@
     )(x0, *atts, *wto_far, wto_own, w_gu, w_down, gain, order)
 
 
-def embed_kernel(tiles, where_ref, parts_ref, mean_ref, gain_ref, win_ref, out_ref):
-    pooled = mean_ref[...]
-    for b in range(parts_ref.shape[0]):
-        pooled = pooled + parts_ref[where_ref[b]]
+def even_sum(refs, first, stride):
+    if stride >= len(refs):
+        return refs[first][...]
+    return even_sum(refs, first, 2 * stride) + even_sum(refs, first + stride, 2 * stride)
+
+
+def embed_kernel(tiles, *refs):
+    mean_ref, gain_ref, win_ref, out_ref = refs[-4:]
+    pooled = mean_ref[...] + even_sum(refs[:-4], 0, 1)
     normed = norm(pooled, gain_ref[2:3, :]).astype(BF16)
     out_ref[...] = mm(normed, win_ref[...])[:tiles].astype(BF16)
 
 
-def embed(where, parts, mean, gain, w_in, tiles):
+def embed(parts, mean, gain, w_in, tiles):
     return pl.pallas_call(
         functools.partial(embed_kernel, tiles),
-        in_specs=[pl.BlockSpec(memory_space=pltpu.SMEM)] + [pl.BlockSpec(memory_space=pltpu.VMEM)] * 4,
+        in_specs=[pl.BlockSpec(memory_space=pltpu.VMEM)] * (len(parts) + 3),
         out_specs=pl.BlockSpec(memory_space=pltpu.VMEM),
         out_shape=jax.ShapeDtypeStruct((tiles, w_in.shape[1]), BF16),
         compiler_params=params(),
         cost_estimate=cost(16 * w_in.shape[0] * w_in.shape[1], 2 * w_in.shape[0] * w_in.shape[1]),
         name="tile_embed",
-    )(where, parts, mean, gain, w_in)
+    )(*parts, mean, gain, w_in)
 
 
 USED = GROUPS * SLIDE_HEAD
 FLAGS = 256 - USED
 SHARE = FLAGS // GROUPS
+
+
+def group_for(pattern_ref, p):
+    group = jnp.int32(0)
+    for g in range(1, GROUPS):
+        group = group + jnp.where(pattern_ref[g] == p, g, 0)
+    return group
 
 
 def between(lane, low, count):
@@ -269,11 +283,11 @@
             w_ref[g, :, 256 : 256 + USED] = w_any[2, :, cut]
             w_ref[g, :, 256 + USED : 256 + 2 * USED] = w_any[1, :, cut]
 
-    hs = norm(x_ref[...].astype(F32), gain_ref[...]).astype(BF16)
+    hs = norm(x_ref[...].astype(F32), gain_ref[...].reshape(1, -1)).astype(BF16)
     wide = hs.astype(F32)
     for c in range(held.shape[0]):
         held[c] = wide[:, c * 128 : (c + 1) * 128]
-    y = mm(hs, w_ref[gid_ref[0]])
+    y = mm(hs, w_ref[group_for(gid_ref, 0)])
     q_refs[0][...] = flagged(y[:, :256] * scale)
     kv0_ref[...] = y[:, 256:].astype(BF16)
     base = 0
@@ -289,7 +303,7 @@
             ],
             axis=1,
         ).astype(BF16)
-        y = mm(rows, w_ref[gid_ref[p]])
+        y = mm(rows, w_ref[group_for(gid_ref, p)])
         lane = lanes((count, y.shape[1])) - FLAGS
         kept = y[0:count]
         for j in range(1, GROUPS):
@@ -308,6 +322,10 @@
 
 def slide_block(rows, ratios):
     return min(rows, 16 * ratios[3])
+
+
+def finish_block(rows, ratios):
+    return min(rows, 2 * slide_block(rows, ratios))
 
 
 def slide_proj(gid, tokens, gain, w, ratios):
@@ -470,31 +488,37 @@
         out_specs=[
             pl.BlockSpec((block, 256), lambda i: (i + first, 0)),
             top_spec,
-        ],
+        ]
+        + ([] if half == 0 else [whole((keys, 256))] * 2),
         out_shape=[
             jax.ShapeDtypeStruct((rows, 256), F32),
             jax.ShapeDtypeStruct((rows // size, FLAGS, size), F32),
-        ],
-        scratch_shapes=[pltpu.VMEM((keys, 256), BF16), pltpu.VMEM((keys, 256), BF16)],
+        ]
+        + ([] if half == 0 else [jax.ShapeDtypeStruct((keys, 256), BF16)] * 2),
+        scratch_shapes=[pltpu.VMEM((keys, 256), BF16), pltpu.VMEM((keys, 256), BF16)] if half == 0 else [],
         input_output_aliases={3 + len(arrays) + i: i for i in range(len(earlier))},
         compiler_params=params(),
         cost_estimate=cost(4 * 4 * done * keys * 256, 2 * keys * 384 + 6 * done * 256, 4 * done * keys),
     )(pos, at, q, *arrays, *earlier)
 
 
-def fresh_kernel(ratios, news, plan, seg_ref, gid_ref, news_ref, emb_ref, pos_ref, gain_ref, w_ref, at_ref, *rest):
-    total = sum(n for n, _, _ in plan)
-    kv_refs = rest[:total]
-    q_ref, sum_ref, top_ref, ka_ref, va_ref, ka, va = rest[total:]
+def fresh_kernel(ratios, news, seg_ref, gid_ref, emb_ref, pos_ref, gain_ref, w_ref, *rest):
+    far_refs = rest[:8]
+    q_ref, sum_ref, top_ref, ka_ref, va_ref, held, queries, sems = rest[8:]
+
+    def fetch(i):
+        return pltpu.make_async_copy(far_refs[i], held.at[i], sems.at[i])
+
+    for i in range(8):
+        fetch(i).start()
     scale = SLIDE_HEAD ** -0.5 * LOG2E
-    hs = norm(emb_ref[...], gain_ref[...]).astype(BF16)
+    hs = norm(emb_ref[...], gain_ref[...].reshape(1, -1)).astype(BF16)
     slots = emb_ref.shape[0]
     pos = pos_ref[...]
     lane = lanes((slots, 256))
     row = lax.broadcasted_iota(jnp.int32, (slots, 256), 0)
-    first = 0
     for p in range(4):
-        y = mm(hs, w_ref[gid_ref[p]])
+        y = mm(hs, w_ref[group_for(gid_ref, p)])
         q = flagged(y[:, :256] * scale)
         kv = y[:, 256:].astype(BF16)
         span = ratios[p] * seg_ref[1]
@@ -510,25 +534,28 @@
             ka_ref[p, h * slots : (h + 1) * slots] = key
             va_ref[p, h * slots : (h + 1) * slots] = jnp.where(between(lane, SLIDE_HEAD * h, SLIDE_HEAD), kv[:, 0:256], none)
         q_ref[p] = q.astype(F32)
-        count, used, cuts = plan[p]
-        refs = kv_refs[first : first + count]
-        first += count
-        augment(loaders([refs[u] for u in used], cuts), at_ref[p], ratios[p], news_ref, news, ka, va)
-        sums, tops = attend_stacked(q, ka, va)
+        queries[p] = q
+
+    def pattern(p, carry):
+        for i in range(2):
+            spot = 2 * p + i
+            pltpu.make_async_copy(far_refs[0], held.at[spot], sems.at[spot]).wait()
+        sums, tops = attend_stacked(queries[p], held.at[2 * p], held.at[2 * p + 1])
         sum_ref[p] = sums
         top_ref[p] = tops
-
-
-def fresh(seg, gid, news_pos, emb, pos, gain, w, at, kvs, ratios):
+        return carry
+
+    lax.fori_loop(0, 4, pattern, 0)
+
+
+def fresh(seg, gid, emb, pos, gain, w, augmented, ratios, news):
     slots = emb.shape[0]
-    keys = at.shape[-1]
+    keys = augmented[0].shape[0]
     smem = pl.BlockSpec(memory_space=pltpu.SMEM)
     vmem = pl.BlockSpec(memory_space=pltpu.VMEM)
-    plan = [(len(arrays), used, cuts) for arrays, used, cuts in kvs]
-    flat = [a for arrays, _, _ in kvs for a in arrays]
     return pl.pallas_call(
-        functools.partial(fresh_kernel, ratios, news_pos.shape[0], plan),
-        in_specs=[smem] * 3 + [vmem] * (5 + len(flat)),
+        functools.partial(fresh_kernel, ratios, news),
+        in_specs=[smem] * 2 + [vmem] * 4 + [pl.BlockSpec(memory_space=pl.ANY)] * 8,
         out_specs=[vmem] * 5,
         out_shape=[
             jax.ShapeDtypeStruct((4, slots, 256), F32),
@@ -537,11 +564,15 @@
             jax.ShapeDtypeStruct((4, GROUPS * slots, 256), BF16),
             jax.ShapeDtypeStruct((4, GROUPS * slots, 256), BF16),
         ],
-        scratch_shapes=[pltpu.VMEM((keys, 256), BF16), pltpu.VMEM((keys, 256), BF16)],
+        scratch_shapes=[
+            pltpu.VMEM((8, keys, 256), BF16),
+            pltpu.VMEM((4, slots, 256), BF16),
+            pltpu.SemaphoreType.DMA((8,)),
+        ],
         compiler_params=params(),
-        cost_estimate=cost(4 * 4 * 4 * slots * keys * 256, 2 * w.size + 8 * keys * 384, 16 * slots * keys),
+        cost_estimate=cost(4 * 4 * 4 * slots * keys * 256, 2 * w.size + 16 * keys * 256, 16 * slots * keys),
         name="slide_fresh",
-    )(seg, gid, news_pos, emb, pos, gain, w, at, *flat)
+    )(seg, gid, emb, pos, gain, w, *augmented)
 
 
 def finish_kernel(ratios, news, gid_ref, start_ref, pos_ref, x_ref, emb_ref, wso_ref, *rest):
@@ -605,50 +636,53 @@
     slots = nka_ref.shape[1] // GROUPS
     owner = lanes((24, 256)) // SLIDE_HEAD
     spread = jnp.where(owner == lax.rem(lax.broadcasted_iota(jnp.int32, (24, 256), 0), 8), 1.0, 0.0).astype(BF16)
-    result = seq[...]
+    scores = [mmt(nka_ref[p], qs[p][...].astype(BF16)) for p in range(4)]
+    weights, splits = [], []
     for p in range(4):
         count = block // ratios[p]
-        s = mmt(nka_ref[p], qs[p][...].astype(BF16))
-        weights = []
         scale = jnp.zeros((8, count), F32)
         line = lax.broadcasted_iota(jnp.int32, (8, count), 0)
+        parts = []
         for h in range(GROUPS):
-            own = s[h * slots : (h + 1) * slots]
+            own = scores[p][h * slots : (h + 1) * slots]
             total = ts[p][SHARE * h : SHARE * h + 1]
             old = ts[p][SHARE * h + 8 : SHARE * h + 9]
             top = jnp.maximum(old, jnp.max(own, axis=0, keepdims=True))
             e = jnp.exp2(own - top)
             shrink = jnp.exp2(old - top)
             inverse = 1.0 / (total * shrink + jnp.sum(e, axis=0, keepdims=True))
-            weights.append((e * inverse).astype(BF16))
+            parts.append((e * inverse).astype(BF16))
             scale = jnp.where(line == h, shrink * inverse, scale)
-        o = lax.dot_general(
-            jnp.concatenate(weights, axis=0), nva_ref[p], (((0,), (0,)), ((), ())), preferred_element_type=F32
-        )
-        high = scale.astype(BF16)
-        rest_one = scale - high.astype(F32)
-        middle = rest_one.astype(BF16)
-        low = (rest_one - middle.astype(F32)).astype(BF16)
-        split = jnp.concatenate([high.astype(F32), middle.astype(F32), low.astype(F32)], axis=0).astype(BF16)
-        wide = lax.dot_general(split, spread, (((0,), (0,)), ((), ())), preferred_element_type=F32)
-        value = ss[p][...] * wide + o
-        if ratios[p] == 1:
-            att = value[:, :USED].astype(BF16)
-        else:
-            lane_wide = lanes((count, 256))
-            for j in range(GROUPS):
-                own = jnp.where(between(lane_wide, SLIDE_HEAD * j, SLIDE_HEAD), value, 0.0)
-                for c in range(2):
-                    at = pl.ds(j, count, stride=ratios[p])
-                    placed[p - 1][c, at, :] = own[:, c * 128 : (c + 1) * 128]
-            att = jnp.concatenate([placed[p - 1][0], placed[p - 1][1]], axis=1)[:, :USED].astype(BF16)
-        result = result + mm(att, wso_ref[gid_ref[p]])
+        weights.append(jnp.concatenate(parts, axis=0))
+        high = scale.astype(BF16).astype(F32)
+        middle = (scale - high).astype(BF16).astype(F32)
+        splits.append(jnp.concatenate([high, middle, scale - high - middle], axis=0).astype(BF16))
+    first = (((0,), (0,)), ((), ()))
+    outs = [
+        lax.dot_general(weights[p], nva_ref[p], first, preferred_element_type=F32) for p in range(4)
+    ]
+    wides = [lax.dot_general(splits[p], spread, first, preferred_element_type=F32) for p in range(4)]
+    values = [ss[p][...] * wides[p] + outs[p] for p in range(4)]
+    for p in range(1, 4):
+        count = block // ratios[p]
+        lane_wide = lanes((count, 256))
+        for j in range(GROUPS):
+            own = jnp.where(between(lane_wide, SLIDE_HEAD * j, SLIDE_HEAD), values[p], 0.0)
+            for c in range(2):
+                at = pl.ds(j, count, stride=ratios[p])
+                placed[p - 1][c, at, :] = own[:, c * 128 : (c + 1) * 128]
+    atts = [values[0][:, :USED].astype(BF16)] + [
+        jnp.concatenate([placed[p - 1][0], placed[p - 1][1]], axis=1)[:, :USED].astype(BF16) for p in range(1, 4)
+    ]
+    result = seq[...]
+    for p in range(4):
+        result = result + mm(atts[p], wso_ref[group_for(gid_ref, p)])
     out_ref[...] = result.astype(BF16)
 
 
 def finish(gid, start, pos, tokens, emb, wso, qs, sums, tops, new, ratios, news):
     rows, width = tokens.shape
-    block = slide_block(rows, ratios)
+    block = finish_block(rows, ratios)
     counts = [block // r for r in ratios]
 
     def rowblock(n, lanes_here):
@@ -746,13 +780,8 @@
 
     patches = gather_shifts(tile_patches, "dev", devs)
 
-    gid = jnp.sum(
-        jnp.where(
-            pattern_of_group[None, :] == lax.iota(jnp.int32, 4)[:, None], lax.iota(jnp.int32, GROUPS)[None, :], 0
-        ),
-        axis=1,
-    ).astype(jnp.int32)
-    gain_row = slide_gain.reshape(1, width)
+    gid = pattern_of_group
+    gain_row = slide_gain
     q0, q1, q2, q3, kv0, kv_near, kv_far, w_slide = slide_proj(gid, slide_tokens, gain_row, w_sqkv, ratios)
     qs = [q0, q1, q2, q3]
 
@@ -829,19 +858,19 @@
     )
     at = after(at, *patches)
 
-    block = slide_block(rows, ratios)
+    block = finish_block(rows, ratios)
     first_half = slide_attend(new_positions, at[0], after(q0, att), kvs[0], 1, block, 0)
     states = [slide_attend(new_positions, at[0], q0, kvs[0], 1, block, 1, first_half)]
-    x0 = after(x0, *states[0])
+    x0 = after(x0, states[0][0])
     for p in range(1, 4):
         states.append(slide_attend(new_positions, at[p], qs[p], kvs[p], ratios[p], block // ratios[p]))
-    sums = [a for a, _ in states]
-    tops = [b for _, b in states]
-
-    pooled = tile_back(x0, atts, w_to, far, w_gu, w_down, tile_gain, order)
-    parts = jnp.stack(gather_shifts(pooled[0], "dev", devs))
+    sums = [state[0] for state in states]
+    tops = [state[1] for state in states]
+
+    part, mean = tile_back(x0, atts, w_to, far, w_gu, w_down, tile_gain, order)
+    parts = gather_shifts(part, "dev", devs)
     tiles = x0.shape[0] // PATCHES
-    tile_embed = embed(ring_dev, parts, pooled[1], tile_gain, w_in, tiles)
+    tile_embed = embed(parts, mean, tile_gain, w_in, tiles)
     every = [tile_embed]
     tags = [0]
     for bit in bits:
@@ -855,7 +884,8 @@
     padded = jnp.pad(every, ((0, slots - news), (0, 0))).astype(F32)
     pos_column = jnp.pad(new_here, (0, slots - news)).reshape(slots, 1)
     seg = jnp.stack([place * rows, jnp.int32(rows)]).astype(jnp.int32)
-    new = fresh(seg, gid, new_positions, padded, pos_column, gain_row, w_slide, at, kvs, ratios)
+    augmented = [a for state in states for a in state[2:]]
+    new = fresh(seg, gid, padded, pos_column, gain_row, w_slide, augmented, ratios, news)
     start = (place * rows).reshape(1).astype(jnp.int32)
     slide_out = finish(
         gid,

time: 231 us -> 222 us (0.961)
  starting transfers between devices: 42.6 us -> 48.4 us
  waiting for transfers between devices: 42.1 us -> 36.6 us
  Pallas kernels: 125 us -> 120 us
  local copies, waits for them, and re-layouts: 13 us -> 9.4 us
    pallas_call x1, Pallas kernels: 17.1 us -> 12.6 us  [finish(): pl.pallas_call(functools.partial(finish_kernel, ratios, news), grid_spec=...]
    ppermute x2, starting transfers between devices: 8.22 us -> 12.6 us  [gather_line(): right = lax.ppermute(x, axis, [(0, 1), (1, 2), (2, 3)])]
    unnamed x54 -> x48, local copies, waits for them, and re-layouts: 5.06 us -> 4.76 us
  transfers between devices with their start and end apart: 34 -> 34, of which waited for: 9 -> 8; matrix products, arithmetic and copies ran while one was open for 6% -> 5% of each run, Pallas kernels for 32% -> 42%
where the time goes in v1:
time: 222 us; the launch traced here: 221 us
  Pallas kernels  120 us (54%)
  starting transfers between devices  48.4 us (22%)
  waiting for transfers between devices  36.6 us (16%)
  local copies, waits for them, and re-layouts  9.4 us (4%)
  other arithmetic  5.58 us (3%)
    pallas_call x5, Pallas kernels, slide_attend(): pl.pallas_call(functools.partial(slide_attend_kernel, ratio, pos.shape[0]...  47.3 us
    ppermute x2, waiting for transfers between devices, gather_line(): across = lax.ppermute(ends, axis, [(0, 3), (3, 0)])  18.8 us
    pallas_call x1, Pallas kernels, tile_back(): pl.pallas_call(functools.partial(tile_back_kernel, devs, pieces), grid=(t...  17.8 us
    pallas_call x1, Pallas kernels, slide_proj(): pl.pallas_call(functools.partial(slide_proj_kernel, ratios), grid_spec=pl...  15.3 us
    pallas_call x1, Pallas kernels, tile_front(): pl.pallas_call(functools.partial(tile_front_kernel, devs), grid=(tokens /...  13.9 us
    ppermute x9, starting transfers between devices, shifted(): return lax.ppermute(x, axis, [(i, (i + by) % size) for i in range(size)])  13.2 us
    pallas_call x1, Pallas kernels, finish(): pl.pallas_call(functools.partial(finish_kernel, ratios, news), grid_spec=...  12.6 us
    ppermute x2, starting transfers between devices, gather_line(): right = lax.ppermute(x, axis, [(0, 1), (1, 2), (2, 3)])  12.6 us
  transfers between devices with their start and end apart: 34, of which 8 were waited for; matrix products, arithmetic and copies ran while one was open for 5% of the time, Pallas kernels for 42%

profile of v1, /device:TPU:0, one launch (start us, length us, event | category | flops | bytes accessed | tf_op | source)
XLA Modules:
  0.0 220.9 jit_solution(8513462274256630189)
XLA Ops:
  0.6 3.1 %collective-permute-start = (bf16[192,588]{1,0:T(8,128)(2,1)}, bf16[192,588]{1,0:T(8,128)(2,1)S(1)}, u32[]{:S(2)}, u32[]{:S(2)}) collective-permute-start(bf16[192,588]{1,0:T(8,128)(2,1)} %rest_0_.1), channel_id=1, source_target_pairs={{0,1},{1,2},{2,3},{3,0},{4,5},{5,6},{6,7},{7,4},{8,9},{9,10},{10,1... | collective-permute-start | bytes 677384 | tf_op jit(solution)/shard_map/ppermute | solution.py:716
  3.7 2.6 %collective-permute-start.1 = (bf16[192,588]{1,0:T(8,128)(2,1)}, bf16[192,588]{1,0:T(8,128)(2,1)S(1)}, u32[]{:S(2)}, u32[]{:S(2)}) collective-permute-start(bf16[192,588]{1,0:T(8,128)(2,1)} %rest_0_.1), channel_id=1, source_target_pairs={{0,2},{1,3},{2,0},{3,1},{4,6},{5,7},{6,4},{7,5},{8,10},{9,11},{10,... | collective-permute-start | bytes 677384 | tf_op jit(solution)/shard_map/ppermute | solution.py:716
  8.6 15.3 %slide_proj.1 = (bf16[2048,256]{1,0:T(8,128)(2,1)}, bf16[512,256]{1,0:T(8,128)(2,1)}, bf16[256,256]{1,0:T(8,128)(2,1)}, bf16[64,256]{1,0:T(8,128)(2,1)}, bf16[20...) custom-call(s32[4]{0:T(128)} %gid_ref.5, ...), custom_call_target="tpu_custom_call" | custom-call | flops 5234491392 | bytes 12976128 | tf_op jit(solution)/shard_map/slide_proj/pallas_call | solution.py:336
  25.3 1.7 collective-permute-start.9
  30.7 13.9 %tile_front.1 = (bf16[768,1536]{1,0:T(8,128)(2,1)}, bf16[768,384]{1,0:T(8,128)(2,1)}) custom-call(s32[4]{0:T(128)} %copy-done.19, bf16[192,588]{1,0:T(8,128)(2,1)} %rest_0_.1, bf16[192,588]{1,0:T(8,128)(2,1)} %copy-done.21, bf16[192,588]{1,0:T(8,128)(2,1)} %copy-done.22, bf16[192,588]{1,0:T(8,128)(2,1)} %copy-done.23, bf16[588,1536]{1,0:T(8,128)(2,1)} %rest_4_.1, ...), custom_call_target="tpu_custom_call" | custom-call | flops 4105175040 | bytes 9197568 | tf_op jit(solution)/shard_map/tile_front/pallas_call | solution.py:90
  44.5 8.0 %collective-permute-start.3 = (bf16[768,384]{1,0:T(8,128)(2,1)}, bf16[768,384]{1,0:T(8,128)(2,1)}, u32[]{:S(2)}, u32[]{:S(2)}) collective-permute-start(bf16[768,384]{1,0:T(8,128)(2,1)} %get-tuple-element.48.rest_0_), channel_id=1, source_target_pairs={{0,1},{1,2},{2,3},{4,5},{5,6},{6,7},{8,9},{9,10},{10,11},{12,13},{... | collective-permute-start | bytes 1769480 | tf_op jit(solution)/shard_map/ppermute | solution.py:734
  52.5 3.7 %collective-permute-start.4 = (bf16[768,384]{1,0:T(8,128)(2,1)}, bf16[768,384]{1,0:T(8,128)(2,1)}, u32[]{:S(2)}, u32[]{:S(2)}) collective-permute-start(bf16[768,384]{1,0:T(8,128)(2,1)} %get-tuple-element.48.rest_0_), channel_id=1, source_target_pairs={{0,3},{3,0},{4,7},{7,4},{8,11},{11,8},{12,15},{15,12},{16,19},{19,... | collective-permute-start | bytes 1769480 | tf_op jit(solution)/shard_map/ppermute | solution.py:741
  59.2 4.6 %collective-permute-start.28 = (bf16[768,384]{1,0:T(8,128)(2,1)S(1)}, bf16[768,384]{1,0:T(8,128)(2,1)S(1)}, u32[]{:S(2)}, u32[]{:S(2)}) collective-permute-start(bf16[768,384]{1,0:T(8,128)(2,1)S(1)} %copy-done.12), channel_id=1, source_target_pairs={{0,1},{1,2},{2,3},{4,5},{5,6},{6,7},{8,9},{9,10},{10,11},{12,13},{... | collective-permute-start | bytes 1769480 | tf_op jit(solution)/shard_map/ppermute | solution.py:734
  67.0 11.3 %collective-permute-done.4.rest_2_.rest_5_ = bf16[768,384]{1,0:T(8,128)(2,1)} collective-permute-done((bf16[768,384]{1,0:T(8,128)(2,1)}, bf16[768,384]{1,0:T(8,128)(2,1)}, u32[]{:S(2)}, u32[]{:S(2)}) %collective-permute-start.4) | collective-permute-done | bytes 589856 | tf_op jit(solution)/shard_map/ppermute | solution.py:741
  81.3 13.7 %shard_map.194 = (f32[2048,256]{1,0:T(8,128)}, f32[2,64,1024]{2,1,0:T(8,128)}) custom-call(s32[24]{0:T(128)} %pos_ref.9, s32[1,2048]{1,0:T(1,128)} %get-tuple-element.93.at_ref, bf16[2048,256]{1,0:T(8,128)(2,1)} %get-tuple-element.49.q_ref.rest_0_, bf16[2048,384]{1,0:T(8,128)(2,1)} %get-tuple-element.47.rest_0_), custom_call_target="tpu_custom_call" | custom-call | flops 8589934592 | bytes 3145728 | tf_op jit(solution)/shard_map/pallas_call | solution.py:478
  97.1 7.0 %collective-permute-done.7.rest_4_ = bf16[768,384]{1,0:T(8,128)(2,1)} collective-permute-done((bf16[768,384]{1,0:T(8,128)(2,1)}, bf16[768,384]{1,0:T(8,128)(2,1)}, u32[]{:S(2)}, u32[]{:S(2)}) %collective-permute-start.7) | collective-permute-done | bytes 589856 | tf_op jit(solution)/shard_map/ppermute | solution.py:740
  106.3 14.1 %shard_map.195 = (f32[2048,256]{1,0:T(8,128)}, f32[2,64,1024]{2,1,0:T(8,128)}, bf16[2048,256]{1,0:T(8,128)(2,1)}, bf16[2048,256]{1,0:T(8,128)(2,1)}) custom-call(s32[24]{0:T(128)} %pos_ref.9, s32[1,2048]{1,0:T(1,128)} %get-tuple-element.93.at_ref, bf16[2048,256]{1,0:T(8,128)(2,1)} %get-tuple-element.49.q_ref.rest_0_, ...), custom_call_target="tpu_custom_call", output_to_operand_aliasing={{0}: (4, {}), {1}: (5, {})} | custom-call | flops 8589934592 | bytes 3145728 | tf_op jit(solution)/shard_map/pallas_call | solution.py:478
  120.4 1.9 collective-permute-start.30
  123.5 5.7 %collective-permute-done.13.rest_10_.rest_3_ = bf16[4,64,1536]{2,1,0:T(8,128)(2,1)} collective-permute-done((bf16[4,64,1536]{2,1,0:T(8,128)(2,1)S(1)}, bf16[4,64,1536]{2,1,0:T(8,128)(2,1)}, u32[]{:S(2)}, u32[]{:S(2)}) %collective-permute-start.13) | collective-permute-done | bytes 786464 | tf_op jit(solution)/shard_map/ppermute | solution.py:749
  131.0 7.5 %collective-permute-done.30 = bf16[768,384]{1,0:T(8,128)(2,1)S(1)} collective-permute-done((bf16[768,384]{1,0:T(8,128)(2,1)}, bf16[768,384]{1,0:T(8,128)(2,1)S(1)}, u32[]{:S(2)}, u32[]{:S(2)}) %collective-permute-start.30) | collective-permute-done | bytes 589856 | tf_op jit(solution)/shard_map/ppermute | solution.py:741
  142.5 17.8 %tile_back.1 = (f32[8,1536]{1,0:T(8,128)}, f32[8,1536]{1,0:T(8,128)}) custom-call(bf16[768,1536]{1,0:T(8,128)(2,1)} %get-tuple-element.53.x0_ref, bf16[768,384]{1,0:T(8,128)(2,1)} %get-tuple-element.48.rest_0_, bf16[768,384]{1,0:T(8,128)(2,1)} %collective-permute-done.3.rest_1_, bf16[768,384]{1,0:T(8,128)(2,1)} %collective-permute-done.4.rest_2_.rest_5_, ...), custom_call_target="tpu_custom_call" | custom-call | flops 8455716864 | bytes 18874368 | tf_op jit(solution)/shard_map/tile_back/pallas_call | solution.py:191
  161.3 3.0 %collective-permute-start.20 = (f32[8,1536]{1,0:T(8,128)}, f32[8,1536]{1,0:T(8,128)S(1)}, u32[]{:S(2)}, u32[]{:S(2)}) collective-permute-start(f32[8,1536]{1,0:T(8,128)} %get-tuple-element.55.refs_0_), channel_id=1, source_target_pairs={{0,3},{1,0},{2,1},{3,2},{4,7},{5,4},{6,5},{7,6},{8,11},{9,8},{10,9... | collective-permute-start | bytes 147464 | tf_op jit(solution)/shard_map/ppermute | solution.py:716
  164.3 2.9 %collective-permute-done.18.refs_1_ = f32[8,1536]{1,0:T(8,128)S(1)} collective-permute-done((f32[8,1536]{1,0:T(8,128)}, f32[8,1536]{1,0:T(8,128)S(1)}, u32[]{:S(2)}, u32[]{:S(2)}) %collective-permute-start.18) | collective-permute-done | bytes 49184 | tf_op jit(solution)/shard_map/ppermute | solution.py:716
  168.5 3.0 %tile_embed.1 = bf16[3,768]{1,0:T(4,128)(2,1)} custom-call(f32[8,1536]{1,0:T(8,128)} %get-tuple-element.55.refs_0_, f32[8,1536]{1,0:T(8,128)} %copy-done.13, f32[8,1536]{1,0:T(8,128)} %copy-done.14, f32[8,1536]{1,0:T(8,128)} %copy-done.15, f32[8,1536]{1,0:T(8,128)} %get-tuple-element.56.refs_4_, f32[3,1536]{1,0:T(4,128)} %refs_5_.1, bf16[1536,768]{1,0:T(8,128)(2,1)} %refs_6_.1), custom_call_target="tpu_custom_call" | custom-call | flops 18874368 | bytes 2359296 | tf_op jit(solution)/shard_map/tile_embed/pallas_call | solution.py:227
  176.9 8.3 %shard_map.196 = (f32[512,256]{1,0:T(8,128)}, f32[2,64,256]{2,1,0:T(8,128)}, bf16[2048,256]{1,0:T(8,128)(2,1)}, bf16[2048,256]{1,0:T(8,128)(2,1)}) custom-call(s32[24]{0:T(128)} %pos_ref.9, s32[1,2048]{1,0:T(1,128)} %get-tuple-element.92.at_ref, bf16[512,256]{1,0:T(8,128)(2,1)} %get-tuple-element.57.q_ref.rest_1_, ...), custom_call_target="tpu_custom_call" | custom-call | flops 4294967296 | bytes 2359296 | tf_op jit(solution)/shard_map/pallas_call | solution.py:478
  186.3 5.6 %shard_map.198 = (f32[64,256]{1,0:T(8,128)}, f32[2,64,32]{2,1,0:T(8,128)}, bf16[2048,256]{1,0:T(8,128)(2,1)}, bf16[2048,256]{1,0:T(8,128)(2,1)}) custom-call(s32[24]{0:T(128)} %pos_ref.9, s32[1,2048]{1,0:T(1,128)} %get-tuple-element.90.at_ref, bf16[64,256]{1,0:T(8,128)(2,1)} %get-tuple-element.59.q_ref.rest_3_, bf16[4,64,1536]{2,1,0:T(8,128)(2,1)} %copy-done, ...), custom_call_target="tpu_custom_call" | custom-call | flops 536870912 | bytes 1671168 | tf_op jit(solution)/shard_map/pallas_call | solution.py:478
  192.9 5.5 %shard_map.197 = (f32[256,256]{1,0:T(8,128)}, f32[2,64,128]{2,1,0:T(8,128)}, bf16[2048,256]{1,0:T(8,128)(2,1)}, bf16[2048,256]{1,0:T(8,128)(2,1)}) custom-call(s32[24]{0:T(128)} %pos_ref.9, s32[1,2048]{1,0:T(1,128)} %get-tuple-element.91.at_ref, bf16[256,256]{1,0:T(8,128)(2,1)} %get-tuple-element.58.q_ref.rest_2_, ...), custom_call_target="tpu_custom_call" | custom-call | flops 2147483648 | bytes 1966080 | tf_op jit(solution)/shard_map/pallas_call | solution.py:478
  198.4 9.7 %slide_fresh.1 = (f32[4,32,256]{2,1,0:T(8,128)}, f32[4,32,256]{2,1,0:T(8,128)}, f32[4,64,32]{2,1,0:T(8,128)}, bf16[4,128,256]{2,1,0:T(8,128)(2,1)}, bf16[4,128,256]{2,1,0:T(8,128)(2,1)}) custom-call(s32[2]{0:T(128)} %pad_add_fusion.2.seg_ref, s32[4]{0:T(128)} %gid_ref.5, f32[32,768]{1,0:T(8,128)} %pad_convert_fusion.emb_ref, s32[32,1]{1,0:T(8,128)} %copy.24.pos_ref, ...), custom_call_target="tpu_custom_call" | custom-call | flops 1073741824 | bytes 12320768 | tf_op jit(solution)/shard_map/slide_fresh/pallas_call | solution.py:556
  208.1 12.6 %slide_finish.1 = bf16[2048,768]{1,0:T(8,128)(2,1)} custom-call(s32[4]{0:T(128)} %gid_ref.5, s32[1]{0:T(128)} %bitcast.6.start_ref, s32[24]{0:T(128)} %copy-done.18, bf16[2048,768]{1,0:T(8,128)(2,1)} %x_ref.3, f32[32,768]{1,0:T(8,128)} %pad_convert_fusion.emb_ref, bf16[4,192,768]{2,1,0:T(8,128)(2,1)} %bitcast.26, ...), custom_call_target="tpu_custom_call" | custom-call | flops 3221225472 | bytes 18874368 | tf_op jit(solution)/shard_map/slide_finish/pallas_call | solution.py:691
  (142 shorter events, 37.1 us)
Async XLA Ops:
  0.6 28.4 %collective-permute-start = (bf16[192,588]{1,0:T(8,128)(2,1)}, bf16[192,588]{1,0:T(8,128)(2,1)S(1)}, u32[]{:S(2)}, u32[]{:S(2)}) collective-permute-start(bf16[192,588]{1,0:T(8,128)(2,1)} %rest_0_.1), channel_id=1, source_target_pairs={{0,1},{1,2},{2,3},{3,0},{4,5},{5,6},{6,7},{7,4},{8,9},{9,10},{10,1... | collective-permute-start | bytes 677384 | tf_op jit(solution)/shard_map/ppermute | solution.py:716
  3.7 25.5 %collective-permute-start.1 = (bf16[192,588]{1,0:T(8,128)(2,1)}, bf16[192,588]{1,0:T(8,128)(2,1)S(1)}, u32[]{:S(2)}, u32[]{:S(2)}) collective-permute-start(bf16[192,588]{1,0:T(8,128)(2,1)} %rest_0_.1), channel_id=1, source_target_pairs={{0,2},{1,3},{2,0},{3,1},{4,6},{5,7},{6,4},{7,5},{8,10},{9,11},{10,... | collective-permute-start | bytes 677384 | tf_op jit(solution)/shard_map/ppermute | solution.py:716
  6.3 22.9 %collective-permute-start.2 = (bf16[192,588]{1,0:T(8,128)(2,1)}, bf16[192,588]{1,0:T(8,128)(2,1)S(1)}, u32[]{:S(2)}, u32[]{:S(2)}) collective-permute-start(bf16[192,588]{1,0:T(8,128)(2,1)} %rest_0_.1), channel_id=1, source_target_pairs={{0,3},{1,0},{2,1},{3,2},{4,7},{5,4},{6,5},{7,6},{8,11},{9,8},{10,9... | collective-permute-start | bytes 677384 | tf_op jit(solution)/shard_map/ppermute | solution.py:716
  24.7 31.5 %collective-permute-start.10 = (bf16[64,1536]{1,0:T(8,128)(2,1)S(1)}, bf16[64,1536]{1,0:T(8,128)(2,1)S(1)}, u32[]{:S(2)}, u32[]{:S(2)}) collective-permute-start(bf16[64,1536]{1,0:T(8,128)(2,1)S(1)} %get-tuple-element.89), channel_id=1, source_target_pairs={{0,3},{1,0},{2,1},{3,2},{4,7},{5,4},{6,5},{7,6},{8,11},{9,8},{10,9... | collective-permute-start | bytes 589832 | tf_op jit(solution)/shard_map/ppermute | solution.py:716
  25.3 32.3 %collective-permute-start.9 = (bf16[64,1536]{1,0:T(8,128)(2,1)S(1)}, bf16[64,1536]{1,0:T(8,128)(2,1)S(1)}, u32[]{:S(2)}, u32[]{:S(2)}) collective-permute-start(bf16[64,1536]{1,0:T(8,128)(2,1)S(1)} %get-tuple-element.89), channel_id=1, source_target_pairs={{0,2},{1,3},{2,0},{3,1},{4,6},{5,7},{6,4},{7,5},{8,10},{9,11},{10,... | collective-permute-start | bytes 589832 | tf_op jit(solution)/shard_map/ppermute | solution.py:716
  29.1 28.4 %collective-permute-start.8 = (bf16[64,1536]{1,0:T(8,128)(2,1)S(1)}, bf16[64,1536]{1,0:T(8,128)(2,1)S(1)}, u32[]{:S(2)}, u32[]{:S(2)}) collective-permute-start(bf16[64,1536]{1,0:T(8,128)(2,1)S(1)} %get-tuple-element.89), channel_id=1, source_target_pairs={{0,1},{1,2},{2,3},{3,0},{4,5},{5,6},{6,7},{7,4},{8,9},{9,10},{10,1... | collective-permute-start | bytes 589832 | tf_op jit(solution)/shard_map/ppermute | solution.py:716
  44.5 21.2 %collective-permute-start.3 = (bf16[768,384]{1,0:T(8,128)(2,1)}, bf16[768,384]{1,0:T(8,128)(2,1)}, u32[]{:S(2)}, u32[]{:S(2)}) collective-permute-start(bf16[768,384]{1,0:T(8,128)(2,1)} %get-tuple-element.48.rest_0_), channel_id=1, source_target_pairs={{0,1},{1,2},{2,3},{4,5},{5,6},{6,7},{8,9},{9,10},{10,11},{12,13},{... | collective-permute-start | bytes 1769480 | tf_op jit(solution)/shard_map/ppermute | solution.py:734
  52.5 25.8 %collective-permute-start.4 = (bf16[768,384]{1,0:T(8,128)(2,1)}, bf16[768,384]{1,0:T(8,128)(2,1)}, u32[]{:S(2)}, u32[]{:S(2)}) collective-permute-start(bf16[768,384]{1,0:T(8,128)(2,1)} %get-tuple-element.48.rest_0_), channel_id=1, source_target_pairs={{0,3},{3,0},{4,7},{7,4},{8,11},{11,8},{12,15},{15,12},{16,19},{19,... | collective-permute-start | bytes 1769480 | tf_op jit(solution)/shard_map/ppermute | solution.py:741
  56.2 23.8 %collective-permute-start.6 = (bf16[768,384]{1,0:T(8,128)(2,1)}, bf16[768,384]{1,0:T(8,128)(2,1)}, u32[]{:S(2)}, u32[]{:S(2)}) collective-permute-start(bf16[768,384]{1,0:T(8,128)(2,1)} %get-tuple-element.48.rest_0_), channel_id=1, source_target_pairs={{3,2},{2,1},{1,0},{7,6},{6,5},{5,4},{11,10},{10,9},{9,8},{15,14},{... | collective-permute-start | bytes 1769480 | tf_op jit(solution)/shard_map/ppermute | solution.py:735
  57.7 39.0 %collective-permute-start.11 = (bf16[4,64,1536]{2,1,0:T(8,128)(2,1)S(1)}, bf16[4,64,1536]{2,1,0:T(8,128)(2,1)S(1)}, u32[]{:S(2)}, u32[]{:S(2)}) collective-permute-start(bf16[4,64,1536]{2,1,0:T(8,128)(2,1)S(1)} %pad_maximum_fusion.rest_7_.rest_0_), channel_id=1, source_target_pairs={{0,8},{4,12},{8,0},{12,4},{16,24},{20,28},{24,16},{28,20},{1,9},{5... | collective-permute-start | bytes 2359304 | tf_op jit(solution)/shard_map/ppermute | solution.py:749
  59.2 35.8 %collective-permute-start.28 = (bf16[768,384]{1,0:T(8,128)(2,1)S(1)}, bf16[768,384]{1,0:T(8,128)(2,1)S(1)}, u32[]{:S(2)}, u32[]{:S(2)}) collective-permute-start(bf16[768,384]{1,0:T(8,128)(2,1)S(1)} %copy-done.12), channel_id=1, source_target_pairs={{0,1},{1,2},{2,3},{4,5},{5,6},{6,7},{8,9},{9,10},{10,11},{12,13},{... | collective-permute-start | bytes 1769480 | tf_op jit(solution)/shard_map/ppermute | solution.py:734
  65.7 31.4 %collective-permute-start.29 = (bf16[768,384]{1,0:T(8,128)(2,1)S(1)}, bf16[768,384]{1,0:T(8,128)(2,1)S(1)}, u32[]{:S(2)}, u32[]{:S(2)}) collective-permute-start(bf16[768,384]{1,0:T(8,128)(2,1)S(1)} %copy-done.12), channel_id=1, source_target_pairs={{3,2},{2,1},{1,0},{7,6},{6,5},{5,4},{11,10},{10,9},{9,8},{15,14},{... | collective-permute-start | bytes 1769480 | tf_op jit(solution)/shard_map/ppermute | solution.py:735
  78.3 18.8 %collective-permute-start.5 = (bf16[768,384]{1,0:T(8,128)(2,1)}, bf16[768,384]{1,0:T(8,128)(2,1)}, u32[]{:S(2)}, u32[]{:S(2)}) collective-permute-start(bf16[768,384]{1,0:T(8,128)(2,1)} %collective-permute-done.3.rest_1_), channel_id=1, source_target_pairs={{1,2},{2,3},{5,6},{6,7},{9,10},{10,11},{13,14},{14,15},{17,18},{18... | collective-permute-start | bytes 1769480 | tf_op jit(solution)/shard_map/ppermute | solution.py:739
  80.0 24.1 %collective-permute-start.7 = (bf16[768,384]{1,0:T(8,128)(2,1)}, bf16[768,384]{1,0:T(8,128)(2,1)}, u32[]{:S(2)}, u32[]{:S(2)}) collective-permute-start(bf16[768,384]{1,0:T(8,128)(2,1)} %collective-permute-done.6.rest_6_), channel_id=1, source_target_pairs={{2,1},{1,0},{6,5},{5,4},{10,9},{9,8},{14,13},{13,12},{18,17},{17,1... | collective-permute-start | bytes 1769480 | tf_op jit(solution)/shard_map/ppermute | solution.py:740
  95.0 28.4 %collective-permute-start.12 = (bf16[4,64,1536]{2,1,0:T(8,128)(2,1)S(1)}, bf16[4,64,1536]{2,1,0:T(8,128)(2,1)}, u32[]{:S(2)}, u32[]{:S(2)}) collective-permute-start(bf16[4,64,1536]{2,1,0:T(8,128)(2,1)S(1)} %pad_maximum_fusion.rest_7_.rest_0_), channel_id=1, source_target_pairs={{0,16},{4,20},{8,24},{12,28},{16,0},{20,4},{24,8},{28,12},{1,17},{... | collective-permute-start | bytes 2359304 | tf_op jit(solution)/shard_map/ppermute | solution.py:749
  96.6 32.6 %collective-permute-start.13 = (bf16[4,64,1536]{2,1,0:T(8,128)(2,1)S(1)}, bf16[4,64,1536]{2,1,0:T(8,128)(2,1)}, u32[]{:S(2)}, u32[]{:S(2)}) collective-permute-start(bf16[4,64,1536]{2,1,0:T(8,128)(2,1)S(1)} %collective-permute-done.11.rest_8_.rest_1_), channel_id=1, source_target_pairs={{0,16},{4,20},{8,24},{12,28},{16,0},{20,4},{24,8},{28,12},{1,17},{... | collective-permute-start | bytes 2359304 | tf_op jit(solution)/shard_map/ppermute | solution.py:749
  104.1 25.2 %collective-permute-start.31 = (bf16[768,384]{1,0:T(8,128)(2,1)S(1)}, bf16[768,384]{1,0:T(8,128)(2,1)S(1)}, u32[]{:S(2)}, u32[]{:S(2)}) collective-permute-start(bf16[768,384]{1,0:T(8,128)(2,1)S(1)} %collective-permute-done.28), channel_id=1, source_target_pairs={{1,2},{2,3},{5,6},{6,7},{9,10},{10,11},{13,14},{14,15},{17,18},{18... | collective-permute-start | bytes 1769480 | tf_op jit(solution)/shard_map/ppermute | solution.py:739
  104.8 25.0 %collective-permute-start.32 = (bf16[768,384]{1,0:T(8,128)(2,1)S(1)}, bf16[768,384]{1,0:T(8,128)(2,1)}, u32[]{:S(2)}, u32[]{:S(2)}) collective-permute-start(bf16[768,384]{1,0:T(8,128)(2,1)S(1)} %collective-permute-done.29), channel_id=1, source_target_pairs={{2,1},{1,0},{6,5},{5,4},{10,9},{9,8},{14,13},{13,12},{18,17},{17,1... | collective-permute-start | bytes 1769480 | tf_op jit(solution)/shard_map/ppermute | solution.py:740
  120.4 18.1 %collective-permute-start.30 = (bf16[768,384]{1,0:T(8,128)(2,1)}, bf16[768,384]{1,0:T(8,128)(2,1)S(1)}, u32[]{:S(2)}, u32[]{:S(2)}) collective-permute-start(bf16[768,384]{1,0:T(8,128)(2,1)} %get-tuple-element.62.rest_0_), channel_id=1, source_target_pairs={{0,3},{3,0},{4,7},{7,4},{8,11},{11,8},{12,15},{15,12},{16,19},{19,... | collective-permute-start | bytes 1769480 | tf_op jit(solution)/shard_map/ppermute | solution.py:741
  123.4 16.4 %collective-permute-start.14 = (bf16[4,64,1536]{2,1,0:T(8,128)(2,1)S(1)}, bf16[4,64,1536]{2,1,0:T(8,128)(2,1)S(1)}, u32[]{:S(2)}, u32[]{:S(2)}) collective-permute-start(bf16[4,64,1536]{2,1,0:T(8,128)(2,1)S(1)} %pad_maximum_fusion.rest_7_.rest_0_), channel_id=1, source_target_pairs={{0,4},{4,0},{8,12},{12,8},{16,20},{20,16},{24,28},{28,24},{1,5},{5... | collective-permute-start | bytes 2359304 | tf_op jit(solution)/shard_map/ppermute | solution.py:749
  129.3 11.5 %collective-permute-start.16 = (bf16[4,64,1536]{2,1,0:T(8,128)(2,1)}, bf16[4,64,1536]{2,1,0:T(8,128)(2,1)S(1)}, u32[]{:S(2)}, u32[]{:S(2)}) collective-permute-start(bf16[4,64,1536]{2,1,0:T(8,128)(2,1)} %collective-permute-done.12.rest_9_.rest_2_), channel_id=1, source_target_pairs={{0,4},{4,0},{8,12},{12,8},{16,20},{20,16},{24,28},{28,24},{1,5},{5... | collective-permute-start | bytes 2359304 | tf_op jit(solution)/shard_map/ppermute | solution.py:749
  129.8 12.8 %collective-permute-start.17 = (bf16[4,64,1536]{2,1,0:T(8,128)(2,1)}, bf16[4,64,1536]{2,1,0:T(8,128)(2,1)}, u32[]{:S(2)}, u32[]{:S(2)}) collective-permute-start(bf16[4,64,1536]{2,1,0:T(8,128)(2,1)} %collective-permute-done.13.rest_10_.rest_3_), channel_id=1, source_target_pairs={{0,4},{4,0},{8,12},{12,8},{16,20},{20,16},{24,28},{28,24},{1,5},{5... | collective-permute-start | bytes 2359304 | tf_op jit(solution)/shard_map/ppermute | solution.py:749
  139.9 53.0 %collective-permute-start.33 = (bf16[4,256,384]{2,1,0:T(8,128)(2,1)}, bf16[4,256,384]{2,1,0:T(8,128)(2,1)}, u32[]{:S(2)}, u32[]{:S(2)}) collective-permute-start(bf16[4,256,384]{2,1,0:T(8,128)(2,1)} %pad_maximum_fusion.1.rest_0_), channel_id=1, source_target_pairs={{0,4},{4,0},{8,12},{12,8},{16,20},{20,16},{24,28},{28,24},{1,5},{5... | collective-permute-start | bytes 2359304 | tf_op jit(solution)/shard_map/ppermute | solution.py:749
  174.2 11.6 %collective-permute-start.22 = (bf16[3,768]{1,0:T(4,128)(2,1)}, bf16[3,768]{1,0:T(4,128)(2,1)S(1)}, u32[]{:S(2)}, u32[]{:S(2)}) collective-permute-start(bf16[3,768]{1,0:T(4,128)(2,1)} %tile_embed.1), channel_id=1, source_target_pairs={{0,16},{4,20},{8,24},{12,28},{16,0},{20,4},{24,8},{28,12},{1,17},{... | collective-permute-start | bytes 13832 | tf_op jit(solution)/shard_map/ppermute | solution.py:749
  (34 other events, 523.8 us)
